TPU v7x, 32 devices: a whole 2x2x4 slice. The times are simulated.
32 devices in a mesh: dp: 8 (over z, y), tensor: 4 (over x, core).
Axes of the slice: x: 2, y: 2, z: 4, core: 2. Of those that a mesh axis runs over, the one named last changes fastest.
Arguments:
- layer_input: bfloat16 [196, 64, 768], P('tensor', 'dp'), may hold values from -6 to 6
- image_counts: int32 [8], P('dp'), may hold values from 4 to 8
- expand: bfloat16 [196, 384], P(None, 'tensor'), may hold values from -0.4375 to 0.4375
- uplift: bfloat16 [384], P('tensor'), may hold values from -3 to 3
- contract: bfloat16 [384, 196], P('tensor'), may hold values from -0.3125 to 0.3125
- offset: bfloat16 [196], P('tensor'), may hold values from -3 to 3
- scaling: bfloat16 [768], replicated, may hold values from 0.099609375 to 1.8984375
- centering: bfloat16 [768], replicated, may hold values from -3 to 3
- rescaling: bfloat16 [768], replicated, may hold values from 0.099609375 to 1.8984375
- recentering: bfloat16 [768], replicated, may hold values from -3 to 3
- broaden: bfloat16 [768, 3072], replicated, may hold values from -0.21875 to 0.21875
- raising: bfloat16 [3072], replicated, may hold values from -3 to 3
- narrow: bfloat16 [3072, 768], replicated, may hold values from -0.109375 to 0.109375
- lowering: bfloat16 [768], replicated, may hold values from -3 to 3
- cotangent: bfloat16 [196, 64, 768], P('tensor', 'dp'), may hold values from -6 to 6
Outputs:
- layer_output: bfloat16 [196, 64, 768], P('tensor', 'dp')
- input_grad: bfloat16 [196, 64, 768], P('tensor', 'dp')
- expand_grad: float32 [196, 384], P(None, 'tensor')
- uplift_grad: float32 [384], P('tensor')
- contract_grad: float32 [384, 196], P('tensor')
- offset_grad: float32 [196], P('tensor')
- scaling_grad: float32 [768], replicated
- centering_grad: float32 [768], replicated
- rescaling_grad: float32 [768], replicated
- recentering_grad: float32 [768], replicated
- broaden_grad: float32 [768, 3072], P(None, ('dp', 'tensor'))
- raising_grad: float32 [3072], P(('dp', 'tensor'))
- narrow_grad: float32 [3072, 768], P(('dp', 'tensor'))
- lowering_grad: float32 [768], replicated
Inputs may be any that keep to these rules, and one draw needn't show every extreme that they name: `image_counts`: slots of a dp index at or above its count hold padding images.
All inputs are finite; a program needn't handle non-finite values.
Results may differ from a plain program's by a relative error of at most 0.007.
Values may be sent and summed in bfloat16 or wider, within the bound.
A program may use at most 128 MiB of HBM per device.

v0:
```python
import jax
import jax.numpy as jnp
from jax import lax
from jax.sharding import PartitionSpec as P


def layer_norm(values, scale_vec, shift_vec):
    centre = values - jnp.mean(values, axis=-1, keepdims=True)
    spread = jnp.mean(centre * centre, axis=-1, keepdims=True)
    return centre * lax.rsqrt(spread + 1e-06) * scale_vec + shift_vec


def local(
    layer_input,
    image_counts,
    expand,
    uplift,
    contract,
    offset,
    scaling,
    centering,
    rescaling,
    recentering,
    broaden,
    raising,
    narrow,
    lowering,
    cotangent,
):
    part_rows, images, model_width = layer_input.shape
    columns = images * model_width
    image_mask = (jnp.arange(images, dtype=jnp.int32) < image_counts[0]).astype(jnp.float32)
    row_mask = jnp.tile(image_mask, part_rows)[:, None]
    input_float = layer_input.astype(jnp.float32)
    normed_first, first_back = jax.vjp(
        layer_norm, input_float, scaling.astype(jnp.float32), centering.astype(jnp.float32)
    )
    normed_local = normed_first.astype(jnp.bfloat16).reshape(part_rows, columns)
    normed_all = lax.all_gather(normed_local, "tensor", axis=0, tiled=True)
    token_pre = (
        jnp.einsum("sj,sn->jn", expand, normed_all, preferred_element_type=jnp.float32)
        + uplift.astype(jnp.float32)[:, None]
    )
    token_act, gelu_token = jax.vjp(jax.nn.gelu, token_pre)
    token_low = token_act.astype(jnp.bfloat16)
    weight_block = contract
    token_out = lax.psum_scatter(
        jnp.einsum("js,jn->sn", weight_block, token_low, preferred_element_type=jnp.float32),
        "tensor",
        scatter_dimension=0,
        tiled=True,
    )
    token_out = token_out + offset.astype(jnp.float32)[:, None]
    mixed_rows = input_float.reshape(part_rows * images, model_width) + token_out.reshape(
        part_rows * images, model_width
    )
    normed_second, second_back = jax.vjp(
        layer_norm, mixed_rows, rescaling.astype(jnp.float32), recentering.astype(jnp.float32)
    )
    normed_low = normed_second.astype(jnp.bfloat16)
    channel_pre = jnp.dot(normed_low, broaden, preferred_element_type=jnp.float32) + raising.astype(
        jnp.float32
    )
    channel_act, gelu_channel = jax.vjp(jax.nn.gelu, channel_pre)
    channel_low = channel_act.astype(jnp.bfloat16)
    channel_out = jnp.dot(
        channel_low, narrow, preferred_element_type=jnp.float32
    ) + lowering.astype(jnp.float32)
    layer_output = (
        ((mixed_rows + channel_out) * row_mask)
        .astype(jnp.bfloat16)
        .reshape(part_rows, images, model_width)
    )
    out_grad = cotangent.astype(jnp.float32).reshape(part_rows * images, model_width) * row_mask
    out_low = out_grad.astype(jnp.bfloat16)
    narrow_grad = jnp.einsum("rk,rd->kd", channel_low, out_low, preferred_element_type=jnp.float32)
    lowering_grad = jnp.sum(out_low.astype(jnp.float32), axis=0)
    act_grad = jnp.einsum("rd,kd->rk", out_low, narrow, preferred_element_type=jnp.float32)
    (pre_grad,) = gelu_channel(act_grad)
    pre_low = pre_grad.astype(jnp.bfloat16)
    broaden_grad = jnp.einsum("rd,rk->dk", normed_low, pre_low, preferred_element_type=jnp.float32)
    raising_grad = jnp.sum(pre_low.astype(jnp.float32), axis=0)
    normed_grad = jnp.einsum("rk,dk->rd", pre_low, broaden, preferred_element_type=jnp.float32)
    rows_grad, rescaling_grad, recentering_grad = second_back(normed_grad)
    mixed_grad = out_grad + rows_grad
    mixed_low = mixed_grad.astype(jnp.bfloat16).reshape(part_rows, columns)
    offset_grad = jnp.sum(mixed_low.astype(jnp.float32), axis=1)
    mixed_all = lax.all_gather(mixed_low, "tensor", axis=0, tiled=True)
    act_token_grad = jnp.einsum(
        "js,sn->jn", contract, mixed_all, preferred_element_type=jnp.float32
    )
    (token_grad,) = gelu_token(act_token_grad)
    token_grad_low = token_grad.astype(jnp.bfloat16)
    expand_grad = jnp.einsum(
        "sn,jn->sj", normed_all, token_grad_low, preferred_element_type=jnp.float32
    )
    contract_grad = jnp.einsum(
        "jn,sn->js", token_low, mixed_all, preferred_element_type=jnp.float32
    )
    uplift_grad = jnp.sum(token_grad_low.astype(jnp.float32), axis=1)
    weight_block = expand
    normed_back = lax.psum_scatter(
        jnp.einsum("sj,jn->sn", weight_block, token_grad_low, preferred_element_type=jnp.float32),
        "tensor",
        scatter_dimension=0,
        tiled=True,
    )
    input_back, scaling_grad, centering_grad = first_back(
        normed_back.reshape(part_rows, images, model_width)
    )
    input_grad = (mixed_grad.reshape(part_rows, images, model_width) + input_back).astype(
        jnp.bfloat16
    )
    expand_grad, uplift_grad, contract_grad, offset_grad = lax.psum(
        (expand_grad, uplift_grad, contract_grad, offset_grad), "dp"
    )
    lowering_grad, scaling_grad, centering_grad, rescaling_grad, recentering_grad = lax.psum(
        (lowering_grad, scaling_grad, centering_grad, rescaling_grad, recentering_grad),
        ("dp", "tensor"),
    )
    broaden_grad, narrow_grad, raising_grad = (
        lax.psum_scatter(broaden_grad, ("dp", "tensor"), scatter_dimension=1, tiled=True),
        lax.psum_scatter(narrow_grad, ("dp", "tensor"), scatter_dimension=0, tiled=True),
        lax.psum_scatter(raising_grad, ("dp", "tensor"), scatter_dimension=0, tiled=True),
    )
    return (
        layer_output,
        input_grad,
        expand_grad,
        uplift_grad,
        contract_grad,
        offset_grad,
        scaling_grad,
        centering_grad,
        rescaling_grad,
        recentering_grad,
        broaden_grad,
        raising_grad,
        narrow_grad,
        lowering_grad,
    )


def solution(mesh):
    in_specs = (
        P("tensor", "dp", None),
        P("dp"),
        P(None, "tensor"),
        P("tensor"),
        P("tensor", None),
        P("tensor"),
        P(),
        P(),
        P(),
        P(),
        P(),
        P(),
        P(),
        P(),
        P("tensor", "dp", None),
    )
    out_specs = (
        P("tensor", "dp", None),
        P("tensor", "dp", None),
        P(None, "tensor"),
        P("tensor"),
        P("tensor", None),
        P("tensor"),
        P(),
        P(),
        P(),
        P(),
        P(None, ("dp", "tensor")),
        P(("dp", "tensor")),
        P(("dp", "tensor"), None),
        P(),
    )
    return jax.shard_map(local, mesh=mesh, in_specs=in_specs, out_specs=out_specs, check_vma=False)
```

profile of v0, /device:TPU:0, one launch (start us, length us, event | category | flops | bytes accessed | tf_op | source)
XLA Modules:
  0.0 556.1 jit_solution(4556848983229731333)
XLA Ops:
  7.3 0.7 convert_element_type.85
  7.9 0.7 convert_element_type.86
  8.6 1.2 convert_reduce_fusion.2
  9.9 1.4 fusion.34
  11.2 1.4 fusion.28
  12.6 1.1 reshape.165
  13.9 29.1 %all-gather.5.cloned.1.call-done = bf16[4,49,6144]{2,1,0:T(8,128)(2,1)} async-done(((bf16[1,49,6144]{2,1,0:T(8,128)(2,1)}), bf16[4,49,6144]{2,1,0:T(8,128)(2,1)}) %all-gather.5.cloned.1.call-update) | async-done | bytes 2408464 | tf_op jit(solution)/shard_map/all_gather | solution.py:39
  42.9 2.5 reshape.166
  45.5 0.5 fusion.2
  46.0 1.4 copy-done.3
  47.4 3.1 convolution_bitcast_fusion.1
  50.6 51.8 %fusion = f32[56,6144]{1,0:T(8,128)} fusion(f32[196,6144]{1,0:T(8,128)} %convolution_bitcast_fusion.1), kind=kCustom, calls=%all-reduce-scatter | all-reduce-scatter fusion | flops 1376257 | bytes 6193664
  102.4 1.1 slice
  103.5 2.1 collective-permute-start
  106.4 0.1 mul.240
  106.5 0.6 dynamic-slice.7
  107.7 8.4 %concatenate = f32[77,6144]{1,0:T(8,128)} concatenate(f32[21,6144]{1,0:T(8,128)} %collective-permute-done, f32[56,6144]{1,0:T(8,128)} %fusion), dimensions={0} | concatenate | bytes 3784704
  116.1 2.7 dynamic-slice_add_fusion
  118.8 2.6 reshape.158
  121.3 1.8 copy.29
  123.1 0.2 fusion.38
  123.3 0.3 multiply_reduce_fusion.2
  123.9 1.7 add_convert_fusion
  125.6 0.8 copy-done.14
  126.4 4.5 fusion.52
  131.0 5.4 convert_reduce_fusion
  136.5 2.4 multiply_reduce_fusion
  138.9 0.6 fusion.51
  139.6 1.1 copy-done.7
  140.6 1.1 convert_reduce_fusion.4
  141.8 2.2 reshape.167
  144.0 0.3 all-reduce.10.cloned.1.call-start
  144.2 34.2 %all-gather.7.cloned.1.call-done = bf16[4,49,6144]{2,1,0:T(8,128)(2,1)} async-done(((bf16[1,49,6144]{2,1,0:T(8,128)(2,1)}), bf16[4,49,6144]{2,1,0:T(8,128)(2,1)}) %all-gather.7.cloned.1.call-update) | async-done | bytes 2408464 | tf_op jit(solution)/shard_map/all_gather | solution.py:88
  178.4 4.0 reshape.168
  182.4 4.3 fusion.48
  186.7 2.1 convert_reduce_fusion.1
  188.8 1.0 copy-done.9
  189.9 1.7 fusion.53
  191.6 9.4 %fusion.41 = f32[3072,768]{1,0:T(8,128)} fusion(bf16[49,8,768]{2,1,0:T(8,128)(2,1)} %param.29, f32[392]{0:T(512)S(1)} %mul.240, f32[392,3072]{1,0:T(8,128)} %copy-done.25, f32[3072]{0:T(1024)S(1)} %convert_element_type.94), kind=kOutput, calls=%fused_computation.69 | convolution fusion | flops 1862633472 | bytes 14870048 | tf_op jit(solution)/shard_map/rk,rd->kd/dot_general | solution.py:76
  201.1 1.0 copy-done.15
  202.1 8.0 %fusion.54 = f32[768,3072]{0,1:T(8,128)} fusion(bf16[392,768]{1,0:T(8,128)(2,1)S(1)} %copy-done.15, bf16[392,3072]{1,0:T(8,128)(2,1)} %copy-done.24), kind=kOutput, calls=%fused_computation.87 | convolution fusion | flops 1849688064 | bytes 12447744 | tf_op jit(solution)/shard_map/rd,rk->dk/dot_general | solution.py:81
  210.1 0.6 copy-done.20
  210.8 0.1 reduce_sum.201
  210.9 0.4 copy-done.10
  211.3 3.1 convolution_bitcast_fusion
  214.4 51.0 %fusion.1 = f32[56,6144]{1,0:T(8,128)S(1)} fusion(f32[196,6144]{1,0:T(8,128)} %convolution_bitcast_fusion), kind=kCustom, calls=%all-reduce-scatter.1 | all-reduce-scatter fusion | flops 1376257 | bytes 6193664
  265.4 0.9 slice.1
  266.3 2.4 collective-permute-start.1
  268.6 7.7 %fusion.26 = bf16[49,8,768]{2,1,0:T(8,128)(2,1)} fusion(bf16[3072,768]{1,0:T(8,128)(2,1)} %param.27, f32[392]{0:T(512)S(1)} %mul.240, f32[768]{0:T(1024)S(1)} %convert_element_type.96, f32[392,768]{1,0:T(8,128)S(1)} %copy-done.6, bf16[49,8,768]{2,1,0:T(8,128)(2,1)S(1)} %copy-done.2, f32[392,3072]{1,0:T(8,128)} %copy-done.25, f32[3072]{0:T(1024)S(1)} %convert_element_type.94), kind=kOutput, calls=%fused_computation.46 | convolution fusion | flops 1863536640 | bytes 11960864 | tf_op jit(solution)/shard_map/dot_general | solution.py:66
  276.4 22.0 %all-reduce.6 = (f32[96]{0:T(128)}, f32[49]{0:T(128)}) all-reduce(f32[96]{0:T(128)S(1)} %get-tuple-element.38, f32[49]{0:T(128)S(1)} %reduce_sum.201), channel_id=1, replica_groups=mesh['dp'=8,'tensor'=4] {'dp'}, use_global_device_ids=true, to_apply=%region_12.0 | all-reduce | flops 145 | bytes 1160 | tf_op jit(solution)/shard_map/psum | solution.py:114
  298.3 7.6 %concatenate.1 = f32[77,6144]{1,0:T(8,128)} concatenate(f32[21,6144]{1,0:T(8,128)} %collective-permute-done.1, f32[56,6144]{1,0:T(8,128)S(1)} %fusion.1), dimensions={0} | concatenate | bytes 3784704
  306.0 1.7 fusion.49
  307.7 0.4 copy.30
  308.1 0.4 fusion.35
  308.5 0.7 fusion.29
  309.2 0.3 copy-done.8
  309.5 0.2 copy-done.13
  309.6 1.5 convert_reduce_fusion.3
  311.2 41.1 %all-reduce.5 = (f32[768]{0:T(1024)}, f32[768]{0:T(1024)}, f32[768]{0:T(1024)}, f32[768]{0:T(1024)}, f32[3072]{0:T(1024)S(1)}, /*index=5*/f32[768]{0:T(1024)}) all-reduce(f32[768]{0:T(1024)S(1)} %get-tuple-element.16, f32[768]{0:T(1024)S(1)} %reduce_sum.205, ...), channel_id=1, replica_groups=mesh['dp'=8,'tensor'=4] {'dp','tensor'}, use_global_device_ids=true, to_apply=%region_18.0 | all-reduce | flops 6912 | bytes 55296 | tf_op jit(solution)/shard_map/psum | solution.py:117
  352.3 0.6 dynamic-slice.4
  352.9 52.7 %reduce-scatter.9.cloned.1.call-done = f32[96,768]{1,0:T(8,128)} async-done(((f32[3072,768]{1,0:T(8,128)}), f32[96,768]{1,0:T(8,128)}) %reduce-scatter.9.cloned.1.call-update) | async-done | bytes 294928 | tf_op jit(solution)/shard_map/reduce_scatter | solution.py:123
  405.5 140.9 %reduce-scatter.7.cloned.1.call-done = f32[768,96]{0,1:T(8,128)} async-done(((f32[768,3072]{0,1:T(8,128)}), f32[768,96]{0,1:T(8,128)}) %reduce-scatter.7.cloned.1.call-update) | async-done | bytes 294928 | tf_op jit(solution)/shard_map/reduce_scatter | solution.py:122
  546.5 1.5 copy.34
  548.0 1.5 copy.35
  (87 shorter events, 0.8 us)
Async XLA Ops:
  7.2 40.2 %copy-start = (bf16[96,196]{1,0:T(8,128)(2,1)S(1)}, bf16[96,196]{1,0:T(8,128)(2,1)}, u32[]{:S(2)}) copy-start(bf16[96,196]{1,0:T(8,128)(2,1)} %param.19) | copy-start | bytes 112900
  7.2 6.6 %copy-start.22 = (bf16[96]{0:T(256)(128)(2,1)S(1)}, bf16[96]{0:T(256)(128)(2,1)}, u32[]{:S(2)}) copy-start(bf16[96]{0:T(256)(128)(2,1)} %param.18) | copy-start | bytes 580
  7.2 35.7 %all-gather.5.cloned.1.call-start = ((), (), s32[]{:S(2)}) async-start(), calls=%async_computation.4 | async-start | bytes 3440640 | tf_op jit(solution)/shard_map/all_gather | solution.py:39
  13.8 164.6 %all-gather.7.cloned.1.call-start = ((), (), s32[]{:S(2)}) async-start(), calls=%async_computation.5 | async-start | bytes 3440640 | tf_op jit(solution)/shard_map/all_gather | solution.py:88
  13.8 31.6 %copy-start.16 = (bf16[196,96]{0,1:T(8,128)(2,1)S(1)}, bf16[196,96]{0,1:T(8,128)(2,1)}, u32[]{:S(2)}) copy-start(bf16[196,96]{0,1:T(8,128)(2,1)} %param.17) | copy-start | bytes 112900
  46.0 1.5 copy-start.3
  50.6 55.7 %copy-start.23 = (bf16[49]{0:T(256)(128)(2,1)S(1)}, bf16[49]{0:T(256)(128)(2,1)}, u32[]{:S(2)}) copy-start(bf16[49]{0:T(256)(128)(2,1)} %param.20) | copy-start | bytes 298
  50.6 55.7 %copy-start.18 = (bf16[768]{0:T(1024)(128)(2,1)S(1)}, bf16[768]{0:T(1024)(128)(2,1)}, u32[]{:S(2)}) copy-start(bf16[768]{0:T(1024)(128)(2,1)} %param.23) | copy-start | bytes 4612
  50.6 55.7 %copy-start.19 = (bf16[768]{0:T(1024)(128)(2,1)S(1)}, bf16[768]{0:T(1024)(128)(2,1)}, u32[]{:S(2)}) copy-start(bf16[768]{0:T(1024)(128)(2,1)} %param.24) | copy-start | bytes 4612
  50.6 55.7 %copy-start.17 = (bf16[3072]{0:T(1024)(128)(2,1)S(1)}, bf16[3072]{0:T(1024)(128)(2,1)}, u32[]{:S(2)}) copy-start(bf16[3072]{0:T(1024)(128)(2,1)} %param.26) | copy-start | bytes 18436
  50.6 55.9 %copy-start.21 = (u32[32]{0:T(128)S(1)}, u32[32]{0:T(128)}, u32[]{:S(2)}) copy-start(u32[32]{0:T(128)} %constant.43) | copy-start | bytes 388
  103.5 4.2 collective-permute-start
  118.8 4.3 copy-start.2
  123.9 7.1 %slice-start.2 = ((s8[4718592]{0:T(1024)(128)(4,1)}), s8[4194304]{0:T(1024)(128)(4,1)S(1)}, s32[]{:S(2)}) async-start(s8[4718592]{0:T(1024)(128)(4,1)} %bitcast.90), calls=%async_computation.9 | async-start | bytes 8388608
  125.6 0.8 copy-start.14
  126.4 4.5 copy-start.12
  126.4 4.6 slice-start.3
  126.4 10.0 %slice-start = ((s8[4718592]{0:T(1024)(128)(4,1)}), s8[4194304]{0:T(1024)(128)(4,1)S(1)}, s32[]{:S(2)}) async-start(s8[4718592]{0:T(1024)(128)(4,1)} %bitcast.88), calls=%async_computation.7 | async-start | bytes 8388608
  131.0 5.4 copy-start.25
  131.0 5.4 copy-start.5
  131.0 5.4 slice-start.1
  136.4 2.5 copy-start.24
  139.5 1.1 copy-start.7
  144.0 208.9 %all-reduce.10.cloned.1.call-start = ((), (), s32[]{:S(2)}) async-start(), calls=%async_computation.6 | async-start | bytes 393216 | tf_op jit(solution)/shard_map/psum | solution.py:114
  182.4 4.3 copy-start.4
  182.4 4.3 copy-start.11
  188.8 1.0 copy-start.9
  191.6 213.9 %reduce-scatter.9.cloned.1.call-start = ((), (), s32[]{:S(2)}) async-start(), calls=%async_computation.3 | async-start | bytes 9732096 | tf_op jit(solution)/shard_map/reduce_scatter | solution.py:123
  201.0 1.1 copy-start.15
  201.0 345.4 %reduce-scatter.7.cloned.1.call-start = ((), (), s32[]{:S(2)}) async-start(), calls=%async_computation.2 | async-start | bytes 9732096 | tf_op jit(solution)/shard_map/reduce_scatter | solution.py:122
  210.1 0.7 copy-start.20
  210.1 1.3 copy-start.10
  214.4 54.2 %copy-start.6 = (f32[392,768]{1,0:T(8,128)S(1)}, f32[392,768]{1,0:T(8,128)}, u32[]{:S(2)}) copy-start(f32[392,768]{1,0:T(8,128)} %reshape.158) | copy-start | bytes 3612676
  266.3 32.1 %collective-permute-start.1 = (f32[21,6144]{1,0:T(8,128)}, f32[21,6144]{1,0:T(8,128)}, u32[]{:S(2)}, u32[]{:S(2)}) collective-permute-start(f32[21,6144]{1,0:T(8,128)} %slice.1), channel_id=1, source_target_pairs={{0,1},{1,2},{2,3},{4,5},{5,6},{6,7},{8,9},{9,10},{10,11},{12,13},{... | collective-permute-start | bytes 1548296
  308.1 1.3 copy-start.8
  308.1 1.5 copy-start.13
  309.2 240.4 %copy-start.1 = (bf16[96,196]{1,0:T(8,128)(2,1)S(1)}, bf16[96,196]{1,0:T(8,128)(2,1)}, u32[]{:S(2)}) copy-start(bf16[96,196]{1,0:T(8,128)(2,1)} %param.19) | copy-start | bytes 112900
Sparse Core Ops, SparseCore 0:
  13.9 28.9 all-gather.4
  144.1 34.2 all-gather.6
  191.7 70.1 all-reduce.9
  269.3 136.2 reduce-scatter.8
  411.8 134.5 reduce-scatter.6
where the time goes:
time: 558 us; the launch traced here: 556 us
  waiting for transfers between devices  257 us (46%)
  blocking collectives  166 us (30%)
  matrix products  52.2 us (9%)
  local copies, waits for them, and re-layouts  44.1 us (8%)
  other arithmetic  16.5 us (3%)
  between operations  15.6 us (3%)
    reduce_scatter x1, waiting for transfers between devices, local(): lax.psum_scatter(broaden_grad, ('dp', 'tensor'), scatter_dimension=1, til...  141 us
    unnamed x2, blocking collectives  103 us
    reduce_scatter x1, waiting for transfers between devices, local(): lax.psum_scatter(narrow_grad, ('dp', 'tensor'), scatter_dimension=0, tile...  52.7 us
    unnamed x74, local copies, waits for them, and re-layouts  41.2 us
    psum x1, blocking collectives, local(): lax.psum((lowering_grad, scaling_grad, centering_grad, rescaling_grad, re...  41.1 us
    all_gather x1, waiting for transfers between devices, local(): mixed_all = lax.all_gather(mixed_low, 'tensor', axis=0, tiled=True)  34.2 us
    all_gather x1, waiting for transfers between devices, local(): normed_all = lax.all_gather(normed_local, 'tensor', axis=0, tiled=True)  29.1 us
    psum x1, blocking collectives, local(): lax.psum((expand_grad, uplift_grad, contract_grad, offset_grad), 'dp')  22 us
  transfers between devices with their start and end apart: 7, of which 4 were waited for; matrix products, arithmetic and copies ran while one was open for 17% of the time, Pallas kernels for 0%

commit v1 on v0

v1 whole, which is shorter than its diff:
```python
import functools

import jax
import jax.numpy as jnp
from jax import lax
from jax.experimental import pallas as pl
from jax.experimental.pallas import tpu as pltpu
from jax.sharding import PartitionSpec as P

MESH = pl.DeviceIdType.MESH
F32 = jnp.float32
BF16 = jnp.bfloat16
EPS = 1e-6


def dot(a, b, ca, cb):
    return lax.dot_general(a, b, (((ca,), (cb,)), ((), ())), preferred_element_type=F32)


def dot_exact(a, b, ca, cb):
    return lax.dot_general(
        a, b, (((ca,), (cb,)), ((), ())), precision=lax.Precision.HIGHEST, preferred_element_type=F32
    )


def gelu_parts(v):
    c = 0.7978845608028654
    v2 = v * v
    t = jnp.tanh(c * v * (1.0 + 0.044715 * v2))
    half = 0.5 + 0.5 * t
    act = v * half
    slope = half + (0.5 * c) * v * (1.0 - t * t) * (1.0 + (3.0 * 0.044715) * v2)
    return act, slope


def norm_stats(v):
    mu = jnp.mean(v, axis=-1, keepdims=True)
    cen = v - mu
    rs = lax.rsqrt(jnp.mean(cen * cen, axis=-1, keepdims=True) + EPS)
    return cen * rs, rs


def norm_back(grad, xhat, rs, gain):
    g = grad * gain
    return rs * (g - jnp.mean(g, axis=-1, keepdims=True) - xhat * jnp.mean(g * xhat, axis=-1, keepdims=True))


class Sizes:
    pass


def kernel(
    z,
    cnt, x, ct_hbm, ex, co, prm, w1_hbm, w2_hbm,
    lo, ig, eg, up, cg, vec, bg, ng,
    ct, w1, w2, xs, sb, rb, et, cc, nb16, tp, ta, mixed, nr, ol, yacc, gacc, mgrad,
    gs, r1, rx0, ry0, rz0, ry1, rz1, rx1, so, ro, so2, ro2,
    vv, vr, ec, ecr, ecs, ecx,
    lsem, a_s, a_r, w_s, w_r, c_s, c_r, x0s, x0r, y0s, y0r, z0s, z0r, y1s, y1r, z1s, z1r, x1s, x1r,
    o_s, o_r, v_s, v_r, e_s, e_r,
):
    D, PT, PP, R, HB, HC, T, NDP = z.D, z.PT, z.PP, z.R, z.HB, z.HC, z.T, z.NDP
    NZ = NDP // 2
    DSL, DS = z.DSL, z.DSL * T
    half_r = R // 2
    dp = lax.axis_index("dp")
    te = lax.axis_index("tensor")
    di = lax.rem(dp, NDP)
    mc = lax.rem(te, 2)
    mx = te // 2
    my = lax.rem(di, 2)
    mz = di // 2

    def tpeer(o):
        if o == 1:
            return te + 1 - 2 * mc
        if o == 2:
            return lax.rem(te + 2, 4)
        return 3 - te

    core_dev = (dp, tpeer(1))
    x_dev = (dp, tpeer(2))
    y_dev = (dp + 1 - 2 * my, te)

    def z_dev(o):
        return (dp - di + lax.rem(di + 2 * o, NDP), te)

    def rc(src, dst, ss, rs, dev):
        return pltpu.make_async_remote_copy(
            src_ref=src, dst_ref=dst, send_sem=ss, recv_sem=rs, device_id=dev, device_id_type=MESH
        )

    lc_ct = pltpu.make_async_copy(ct_hbm, ct, lsem.at[0])
    lc_w1 = pltpu.make_async_copy(w1_hbm, w1, lsem.at[1])
    lc_w2 = pltpu.make_async_copy(w2_hbm, w2, lsem.at[2])
    lc_ct.start()

    peers = [(dp, tpeer(o)) for o in (1, 2, 3)] + [y_dev] + [z_dev(o) for o in range(1, NZ)]
    bar = pltpu.get_barrier_semaphore()
    for dev in peers:
        pl.semaphore_signal(bar, inc=1, device_id=dev, device_id_type=MESH)

    def spread(src, k):
        for c in range(D // 128):
            lanes = slice(c * 128, c * 128 + 128)
            xs[c * PP * 8 : c * PP * 8 + PT * 8, :] = src[:, :, lanes].astype(F32).reshape(PT * 8, 128)
            for j in range(T):
                for b in range(2):
                    piece = xs[pl.ds(c * PP * 8 + 2 * j + b, PP, stride=8), :]
                    sb[k, j, b, :, lanes] = piece.astype(BF16)

    def a2a(k, o, b):
        j = tpeer(o)
        return rc(sb.at[k, j, b], rb.at[k, te, b], a_s.at[k, o - 1, b], a_r.at[k, o - 1, b], (dp, j))

    for c in range(D // 128):
        xs[c * PP * 8 + PT * 8 : (c + 1) * PP * 8, :] = jnp.zeros((PP * 8 - PT * 8, 128), F32)
    spread(x, 0)
    pl.semaphore_wait(bar, len(peers))
    for b in range(2):
        for o in (2, 3, 1):
            a2a(0, o, b).start()
    lc_w1.start()
    lc_w2.start()
    for b in range(2):
        rb[0, te, b] = sb[0, te, b]

    row = lax.broadcasted_iota(jnp.int32, (PT * T, PP * T), 0)
    col = lax.broadcasted_iota(jnp.int32, (PT * T, PP * T), 1)
    pick = jnp.zeros((PT * T, PP * T), F32)
    for t in range(T):
        inside = (col >= PP * t) & (col < PP * t + PT) & (row - PT * t == col - PP * t)
        pick = pick + jnp.where(inside, 1.0, 0.0)
    pick16 = pick.astype(BF16)
    col1 = lax.broadcasted_iota(jnp.int32, (1, PP * T), 1)
    pad_one = jnp.where(col1 == PT, 1.0, 0.0)
    uplift_col = dot_exact(prm[6:7, 0:DSL], pad_one, 0, 0)
    ew = dot(ex[...], pick16, 0, 0) + uplift_col
    cw = dot(co[...], pick16, 1, 0)
    et[te, 0] = ew.astype(BF16)
    et[te, 1] = cw.astype(BF16)
    mine = (col1 >= PP * te) & (col1 < PP * te + PT)
    off_row = jnp.where(mine, prm[5:6, 0 : PP * T], 0.0)
    cc[te] = jnp.broadcast_to(off_row, (8, PP * T))

    def wcopies(o):
        dev = (dp, tpeer(o))
        return (
            rc(et.at[te], et.at[te], w_s.at[0, o - 1], w_r.at[0, o - 1], dev),
            rc(cc.at[te], cc.at[te], w_s.at[1, o - 1], w_r.at[1, o - 1], dev),
        )

    def wrecv(o):
        j = tpeer(o)
        return (
            rc(et.at[j], et.at[j], w_s.at[0, o - 1], w_r.at[0, o - 1], (dp, j)),
            rc(cc.at[j], cc.at[j], w_s.at[1, o - 1], w_r.at[1, o - 1], (dp, j)),
        )

    for o in (2, 3, 1):
        for c in wcopies(o):
            c.start()

    lc_ct.wait()
    spread(ct, 1)
    for b in range(2):
        for o in (2, 3, 1):
            a2a(1, o, b).start()
    for b in range(2):
        rb[1, te, b] = sb[1, te, b]

    def a2a_wait(k, o, b):
        j = tpeer(o)
        rc(sb.at[k, j, b], rb.at[k, j, b], a_s.at[k, o - 1, b], a_r.at[k, o - 1, b], (dp, j)).wait_recv()

    for o in (1, 2, 3):
        for c in wrecv(o):
            c.wait_recv()

    e_t = et[:, 0].reshape(DS, PP * T)
    c_t = et[:, 1].reshape(DS, PP * T)
    zero_pad = lax.broadcasted_iota(jnp.int32, (DS, PP * T), 1) == PT
    e_clean = jnp.where(zero_pad, 0.0, e_t.astype(F32)).astype(BF16)
    off_full = (cc[0] + cc[1]) + (cc[2] + cc[3])
    first8 = lax.broadcasted_iota(jnp.int32, (8, PP * T), 0) == 0
    off_row8 = jnp.where(first8, off_full, 0.0).astype(BF16)
    scaling, centering = prm[0:1, :], prm[1:2, :]
    rescaling, recentering = prm[2:3, :], prm[3:4, :]
    lowering = prm[4:5, :]
    rows_b = lax.broadcasted_iota(jnp.int32, (half_r, 1), 0)
    ones_row = rows_b == PT
    ones8 = jnp.where(lax.broadcasted_iota(jnp.int32, (8, D), 0) == 0, 1.0, 0.0).astype(BF16)

    def image_rows(k, b):
        return jnp.concatenate([rb[k, t, b].astype(F32) for t in range(T)], axis=0)

    for b in range(2):
        for o in (1, 2, 3):
            a2a_wait(0, o, b)
        sl = slice(b * half_r, (b + 1) * half_r)
        xb = image_rows(0, b)
        xhat, _ = norm_stats(xb)
        n = jnp.where(ones_row, 1.0, xhat * scaling + centering).astype(BF16)
        nb16[sl, :] = n
        pre = dot(e_t, n, 1, 0)
        tp[b] = pre
        act, _ = gelu_parts(pre)
        ta[b, 0:DS, :] = act.astype(BF16)
        ta[b, DS : DS + 8, :] = ones8
        tok = dot(c_t, ta[b, 0:DS, :], 0, 0) + dot(off_row8, ones8, 0, 0)
        mx_b = xb + tok
        mixed[sl, :] = mx_b
        xh2, _ = norm_stats(mx_b)
        nr[sl, :] = (xh2 * rescaling + recentering).astype(BF16)

    low_sum = jnp.zeros((1, D), F32)
    for b in range(2):
        for o in (1, 2, 3):
            a2a_wait(1, o, b)
        sl = slice(b * half_r, (b + 1) * half_r)
        keep = jnp.where(2 * te + b < cnt[0], 1.0, 0.0)
        og = image_rows(1, b) * keep
        ol[sl, :] = og.astype(BF16)
        low_sum = low_sum + jnp.sum(og, axis=0, keepdims=True)
    vv[...] = jnp.zeros(vv.shape, F32)
    vv[4:5, :] = low_sum
    yacc[...] = jnp.zeros(yacc.shape, F32)
    gacc[...] = jnp.zeros(gacc.shape, F32)
    lc_w1.wait()
    lc_w2.wait()

    def add_into(dst, src):
        dst[...] = (dst[...].astype(F32) + src[...].astype(F32)).astype(BF16)

    def core_copy(i):
        return rc(gs.at[i, 1 - mc], r1.at[i], c_s.at[i], c_r.at[i], core_dev)

    def x0_copy(i):
        return rc(gs.at[i, mc, 0, 1 - mx], rx0.at[i], x0s.at[i], x0r.at[i], x_dev)

    def y1_copy(i):
        return rc(gs.at[i, mc, 1], ry1.at[i], y1s.at[i], y1r.at[i], y_dev)

    def after_core(i):
        core_copy(i).wait_recv()
        for g in range(2):
            for xx in range(2):
                add_into(gs.at[i, mc, g, xx], r1.at[i, g, xx])
        x0_copy(i).start()

    def block(i, carry):
        other = jnp.where(i < NZ, 1, 0)
        zz = lax.rem(mz + 1 + lax.rem(i, NZ), NZ)
        yy = lax.rem(my + other, 2)
        d = zz * 2 + yy
        cols = pl.ds(pl.multiple_of(d * HB, HB), HB)
        w1d = w1[:, cols]
        w2d = w2[cols, :]
        pre = dot(nr[...], w1d, 1, 0) + prm[pl.ds(8 + d, 1), 0:HB]
        act, slope = gelu_parts(pre)
        act16 = act.astype(BF16)
        back = dot(ol[...], w2d, 1, 1)
        low32 = slope * back
        low16 = low32.astype(BF16)
        yacc[...] += dot(act16, w2d, 1, 0)
        gacc[...] += dot(low16, w1d, 1, 1)
        gn = dot(act16, ol[...], 0, 0)
        gb = dot(low16, nr[...], 0, 0)
        for t in range(T):
            gs[i, t % 2, 0, t // 2] = gn[t * HC : (t + 1) * HC, :].astype(BF16)
            gs[i, t % 2, 1, t // 2] = gb[t * HC : (t + 1) * HC, :].astype(BF16)
        vv[pl.ds(8 + d, 1), 0:HB] = jnp.sum(low16.astype(F32), axis=0, keepdims=True)
        core_copy(i).start()

        @pl.when(i > 0)
        def _():
            after_core(i - 1)

            @pl.when(i - 1 < NZ)
            def _():
                y1_copy(i - 1).start()

        return carry

    lax.fori_loop(0, NDP, block, 0)
    after_core(NDP - 1)

    def ocopy(k, o):
        src, dst = (so, ro) if k == 0 else (so2, ro2)
        j = tpeer(o)
        return rc(src.at[j], dst.at[te], o_s.at[k, o - 1], o_r.at[k, o - 1], (dp, j))

    def ocopy_in(k, o):
        src, dst = (so, ro) if k == 0 else (so2, ro2)
        j = tpeer(o)
        return rc(src.at[j], dst.at[j], o_s.at[k, o - 1], o_r.at[k, o - 1], (dp, j))

    for b in range(2):
        keep = jnp.where(2 * te + b < cnt[0], 1.0, 0.0)
        for t in range(T):
            r0 = b * half_r + t * PP
            sl = slice(r0, r0 + PP)
            so[t, b] = ((mixed[sl, :] + yacc[sl, :] + lowering) * keep).astype(BF16)
    for o in (2, 3, 1):
        ocopy(0, o).start()
    ro[te] = so[te]

    resc_sum = jnp.zeros((1, D), F32)
    rece_sum = jnp.zeros((1, D), F32)
    for b in range(2):
        sl = slice(b * half_r, (b + 1) * half_r)
        xh2, rs2 = norm_stats(mixed[sl, :])
        gr = gacc[sl, :]
        resc_sum = resc_sum + jnp.sum(gr * xh2, axis=0, keepdims=True)
        rece_sum = rece_sum + jnp.sum(gr, axis=0, keepdims=True)
        mgrad[sl, :] = ol[sl, :].astype(F32) + norm_back(gr, xh2, rs2, rescaling)
    vv[2:3, :] = resc_sum
    vv[3:4, :] = rece_sum

    eg_sum = jnp.zeros((DS, PP * T), F32)
    cg_sum = jnp.zeros((DS + 8, PP * T), F32)
    scal_sum = jnp.zeros((1, D), F32)
    cent_sum = jnp.zeros((1, D), F32)
    for b in range(2):
        sl = slice(b * half_r, (b + 1) * half_r)
        ml = mgrad[sl, :].astype(BF16)
        _, slope = gelu_parts(tp[b])
        tg = (slope * dot(c_t, ml, 1, 0)).astype(BF16)
        cg_sum = cg_sum + dot(ta[b], ml, 1, 1)
        eg_sum = eg_sum + dot(tg, nb16[sl, :], 1, 1)
        nback = dot(e_clean, tg, 0, 0)
        xhat, rs1 = norm_stats(image_rows(0, b))
        scal_sum = scal_sum + jnp.sum(nback * xhat, axis=0, keepdims=True)
        cent_sum = cent_sum + jnp.sum(nback, axis=0, keepdims=True)
        grad = (mgrad[sl, :] + norm_back(nback, xhat, rs1, scaling)).astype(BF16)
        for t in range(T):
            so2[t, b] = grad[t * PP : (t + 1) * PP, :]
    for o in (2, 3, 1):
        ocopy(1, o).start()
    ro2[te] = so2[te]
    vv[0:1, :] = scal_sum
    vv[1:2, :] = cent_sum
    vv[5:6, 0 : PP * T] = cg_sum[DS : DS + 1, :]
    for t in range(T):
        ec[t % 2, t // 2, 0] = eg_sum[t * DSL : (t + 1) * DSL, :]
        ec[t % 2, t // 2, 1] = cg_sum[t * DSL : (t + 1) * DSL, :]

    def e_core():
        return rc(ec.at[1 - mc], ecr, e_s.at[0], e_r.at[0], core_dev)

    def v_copy(s, dev):
        return rc(vv, vr.at[s], v_s.at[s], v_r.at[s], dev)

    e_core().start()
    v_copy(0, core_dev).start()
    e_core().wait_recv()
    ecs[0] = (ec[mc, 1 - mx] + ecr[1 - mx]).astype(BF16)
    own_ec = ec[mc, mx] + ecr[mx]

    def e_x():
        return rc(ecs.at[0], ecx.at[0], e_s.at[1], e_r.at[1], x_dev)

    e_x().start()
    v_copy(0, core_dev).wait()
    vv[...] = vv[...] + vr[0]
    v_copy(1, x_dev).start()

    for q in range(NZ):
        y1_copy(q).wait_recv()
        for xx in range(2):
            add_into(gs.at[NZ + q, mc, 1, xx], ry1.at[q, xx])
        if q < NZ - 1:
            rc(gs.at[NZ + q, mc, 1], rz1.at[q], z1s.at[q], z1r.at[q], z_dev(q + 1)).start()

    e_x().wait_recv()
    own_ec = own_ec + ecx[0].astype(F32)
    ecs[1] = own_ec.astype(BF16)

    def e_y():
        return rc(ecs.at[1], ecx.at[1], e_s.at[2], e_r.at[2], y_dev)

    e_y().start()
    v_copy(1, x_dev).wait()
    vv[...] = vv[...] + vr[1]
    v_copy(2, y_dev).start()

    def y0_copy(q):
        return rc(gs.at[q, mc, 0, mx], ry0.at[q], y0s.at[q], y0r.at[q], y_dev)

    for i in range(NDP):
        x0_copy(i).wait_recv()
        add_into(gs.at[i, mc, 0, mx], rx0.at[i])
        if i < NZ:
            y0_copy(i).start()

    e_y().wait_recv()
    own_ec = own_ec + ecx[1].astype(F32)
    ecs[2] = own_ec.astype(BF16)

    def e_z(o):
        return rc(ecs.at[2], ecx.at[1 + o], e_s.at[2 + o], e_r.at[2 + o], z_dev(o))

    def v_z(o):
        return rc(vv, vr.at[2 + o], v_s.at[2 + o], v_r.at[2 + o], z_dev(o))

    for o in range(1, NZ):
        e_z(o).start()
    v_copy(2, y_dev).wait()
    vv[...] = vv[...] + vr[2]
    for o in range(1, NZ):
        v_z(o).start()

    for q in range(NZ):
        y0_copy(q).wait_recv()
        add_into(gs.at[NZ + q, mc, 0, mx], ry0.at[q])
        if q < NZ - 1:
            rc(gs.at[NZ + q, mc, 0, mx], rz0.at[q], z0s.at[q], z0r.at[q], z_dev(q + 1)).start()

    for q in range(NZ - 1):
        rc(gs.at[NZ + q, mc, 1], rz1.at[q], z1s.at[q], z1r.at[q], z_dev(q + 1)).wait_recv()

    def z_total(xx):
        tot = gs[NDP - 1, mc, 1, xx].astype(F32)
        for q in range(NZ - 1):
            tot = tot + rz1[q, xx].astype(F32)
        return tot

    r1[0, 0, 0] = z_total(1 - mx).astype(BF16)
    own_b = z_total(mx)
    x1 = rc(r1.at[0, 0, 0], rx1, x1s, x1r, x_dev)
    x1.start()

    def collect(k, dst):
        src = ro if k == 0 else ro2
        for o in (1, 2, 3):
            ocopy_in(k, o).wait_recv()
        for c in range(D // 128):
            lanes = slice(c * 128, c * 128 + 128)
            for j in range(T):
                for b in range(2):
                    xs[pl.ds(c * PP * 8 + 2 * j + b, PP, stride=8), :] = src[j, b, :, lanes].astype(F32)
            dst[:, :, lanes] = xs[c * PP * 8 : c * PP * 8 + PT * 8, :].reshape(PT, 8, 128).astype(BF16)

    collect(0, lo)
    collect(1, ig)

    for o in range(1, NZ):
        e_z(o).wait_recv()
        v_z(o).wait_recv()
    tot_ec = own_ec
    tot_v = vv[...]
    for o in range(1, NZ):
        tot_ec = tot_ec + ecx[1 + o].astype(F32)
        tot_v = tot_v + vr[2 + o]
    vec[...] = tot_v
    eg[...] = dot_exact(pick, tot_ec[0], 1, 1)
    cg[...] = dot_exact(tot_ec[1], pick, 1, 1)
    up[...] = dot_exact(jnp.broadcast_to(pad_one, (8, PP * T)), tot_ec[0], 1, 1)

    for q in range(NZ - 1):
        rc(gs.at[NZ + q, mc, 0, mx], rz0.at[q], z0s.at[q], z0r.at[q], z_dev(q + 1)).wait_recv()
    tot = gs[NDP - 1, mc, 0, mx].astype(F32)
    for q in range(NZ - 1):
        tot = tot + rz0[q].astype(F32)
    ng[...] = tot
    x1.wait_recv()
    bg[...] = jnp.transpose(own_b + rx1[...].astype(F32))

    for k in range(2):
        for o in (1, 2, 3):
            for b in range(2):
                a2a(k, o, b).wait_send()
            ocopy(k, o).wait_send()
    for o in (1, 2, 3):
        for c in wcopies(o):
            c.wait_send()
    for i in range(NDP):
        core_copy(i).wait_send()
        x0_copy(i).wait_send()
    for q in range(NZ):
        y1_copy(q).wait_send()
        y0_copy(q).wait_send()
    for q in range(NZ - 1):
        rc(gs.at[NZ + q, mc, 1], rz1.at[q], z1s.at[q], z1r.at[q], z_dev(q + 1)).wait_send()
        rc(gs.at[NZ + q, mc, 0, mx], rz0.at[q], z0s.at[q], z0r.at[q], z_dev(q + 1)).wait_send()
    x1.wait_send()
    e_core().wait_send()
    e_x().wait_send()
    e_y().wait_send()
    for o in range(1, NZ):
        e_z(o).wait_send()
        v_z(o).wait_send()


def local(
    layer_input, image_counts, expand, uplift, contract, offset, scaling, centering,
    rescaling, recentering, broaden, raising, narrow, lowering, cotangent, *, mesh,
):
    z = Sizes()
    z.PT, images, z.D = layer_input.shape
    z.T, z.NDP = mesh.shape["tensor"], 8
    outer = mesh.shape["dp"] // z.NDP
    z.PP = -(-(z.PT + 1) // 8) * 8
    z.R = 2 * z.T * z.PP
    hidden = broaden.shape[1]
    if outer > 1:
        split = (outer, z.NDP, z.T, hidden // (outer * z.NDP * z.T))
        broaden = broaden.reshape(-1, *split).transpose(0, 2, 3, 1, 4).reshape(-1, hidden)
        raising = raising.reshape(split).transpose(1, 2, 0, 3).reshape(hidden)
        narrow = narrow.reshape(*split, -1).transpose(1, 2, 0, 3, 4).reshape(hidden, -1)
    z.HB = hidden // z.NDP
    z.HC = z.HB // z.T
    z.DSL = expand.shape[1]
    D, T, NDP, PP, PT, R, HB, HC, DSL = z.D, z.T, z.NDP, z.PP, z.PT, z.R, z.HB, z.HC, z.DSL
    DS, NZ = DSL * T, NDP // 2

    def line(v):
        return jnp.pad(v.astype(F32), (0, D - v.shape[0]))[None]

    off_line = jnp.tile(jnp.pad(offset.astype(F32), (0, PP - PT)), T)
    prm = jnp.concatenate(
        [line(v) for v in (scaling, centering, rescaling, recentering, lowering, off_line, uplift)]
        + [jnp.zeros((1, D), F32), jnp.pad(raising.astype(F32).reshape(NDP, HB), ((0, 0), (0, D - HB)))],
        axis=0,
    )
    vm = pl.BlockSpec(memory_space=pltpu.VMEM)
    anys = pl.BlockSpec(memory_space=pl.ANY)
    dma = pltpu.SemaphoreType.DMA
    V = pltpu.VMEM
    scratch = [
        V((PT, 8, D), BF16), V(broaden.shape, BF16), V(narrow.shape, BF16), V((D // 128 * PP * 8, 128), F32),
        V((2, T, 2, PP, D), BF16), V((2, T, 2, PP, D), BF16), V((T, 2, DSL, PP * T), BF16), V((T, 8, PP * T), F32),
        V((R, D), BF16), V((2, DS, D), F32), V((2, DS + 8, D), BF16), V((R, D), F32), V((R, D), BF16), V((R, D), BF16),
        V((R, D), F32), V((R, D), F32), V((R, D), F32),
        V((NDP, 2, 2, 2, HC, D), BF16), V((NDP, 2, 2, HC, D), BF16), V((NDP, HC, D), BF16), V((NZ, HC, D), BF16),
        V((NZ - 1, HC, D), BF16), V((NZ, 2, HC, D), BF16), V((NZ - 1, 2, HC, D), BF16), V((HC, D), BF16),
        V((T, 2, PP, D), BF16), V((T, 2, PP, D), BF16), V((T, 2, PP, D), BF16), V((T, 2, PP, D), BF16),
        V((16, D), F32), V((2 + NZ, 16, D), F32), V((2, 2, 2, DSL, PP * T), F32), V((2, 2, DSL, PP * T), F32),
        V((3, 2, DSL, PP * T), BF16), V((1 + NZ, 2, DSL, PP * T), BF16),
        dma((3,)), dma((2, 3, 2)), dma((2, 3, 2)), dma((2, 3)), dma((2, 3)), dma((NDP,)), dma((NDP,)),
        dma((NDP,)), dma((NDP,)), dma((NZ,)), dma((NZ,)), dma((NZ - 1,)), dma((NZ - 1,)),
        dma((NZ,)), dma((NZ,)), dma((NZ - 1,)), dma((NZ - 1,)), dma(()), dma(()),
        dma((2, 3)), dma((2, 3)), dma((2 + NZ,)), dma((2 + NZ,)), dma((2 + NZ,)), dma((2 + NZ,)),
    ]
    S = jax.ShapeDtypeStruct
    outs = pl.pallas_call(
        functools.partial(kernel, z),
        out_shape=(
            S((PT, images, D), BF16), S((PT, images, D), BF16), S((PT * T, DSL), F32), S((8, DSL), F32),
            S((DSL, PT * T), F32), S((16, D), F32), S((D, HC), F32), S((HC, D), F32),
        ),
        in_specs=[pl.BlockSpec(memory_space=pltpu.SMEM), vm, anys, vm, vm, vm, anys, anys],
        out_specs=(vm,) * 8,
        scratch_shapes=scratch,
        compiler_params=pltpu.CompilerParams(
            collective_id=0, has_side_effects=True, vmem_limit_bytes=62 * 1024 * 1024
        ),
    )(image_counts, layer_input, cotangent, expand, contract, prm, broaden, narrow)
    lo, ig, eg, up, cg, vec, bg, ng = outs
    te, dp = lax.axis_index("tensor"), lax.rem(lax.axis_index("dp"), NDP)
    off = lax.dynamic_slice(vec, (5, te * PP), (1, PT))[0]
    rg = lax.dynamic_slice(vec, (8 + dp, te * HC), (1, HC))[0]
    if outer > 1:
        same = [[o * NDP + i for o in range(outer)] for i in range(NDP)]
        eg, up, cg, off, vec = lax.psum((eg, up, cg, off, vec), "dp", axis_index_groups=same)
        bg = lax.psum_scatter(bg.T, "dp", scatter_dimension=0, axis_index_groups=same, tiled=True).T
        ng = lax.psum_scatter(ng, "dp", scatter_dimension=0, axis_index_groups=same, tiled=True)
        rg = lax.psum_scatter(rg, "dp", scatter_dimension=0, axis_index_groups=same, tiled=True)
    return lo, ig, eg, up[0], cg, off, vec[0], vec[1], vec[2], vec[3], bg, rg, ng, vec[4]


def solution(mesh):
    rows = P("tensor", "dp", None)
    both = ("dp", "tensor")
    in_specs = (
        rows, P("dp"), P(None, "tensor"), P("tensor"), P("tensor", None), P("tensor"),
        P(), P(), P(), P(), P(), P(), P(), P(), rows,
    )
    out_specs = (
        rows, rows, P(None, "tensor"), P("tensor"), P("tensor", None), P("tensor"),
        P(), P(), P(), P(), P(None, both), P(both), P(both, None), P(),
    )
    return jax.shard_map(
        functools.partial(local, mesh=mesh), mesh=mesh, in_specs=in_specs, out_specs=out_specs, check_vma=False
    )
```

time: 558 us -> 133 us (0.24)
  waiting for transfers between devices: 257 us -> 0 us
  blocking collectives: 166 us -> 0 us
  Pallas kernels: 0 us -> 107 us
  matrix products: 52.2 us -> 0 us
  local copies, waits for them, and re-layouts: 44.1 us -> 21.8 us
  other arithmetic: 16.5 us -> 1.32 us
  between operations: 15.6 us -> 1.33 us
    reduce_scatter x2 -> x0, waiting for transfers between devices: 194 us -> none  [the longest x1 141 us: local(): lax.psum_scatter(broaden_grad, ('dp', 'tensor'), scatter_dimension=1, til...]
    pallas_call x0 -> x1, Pallas kernels: none -> 107 us  [local(): pl.pallas_call(functools.partial(kernel, z), out_shape=(S((PT, images, D)...]
    unnamed x2 -> x0, blocking collectives: 103 us -> none
    all_gather x2 -> x0, waiting for transfers between devices: 63.2 us -> none  [the longest x1 34.2 us: local(): mixed_all = lax.all_gather(mixed_low, 'tensor', axis=0, tiled=True)]
    psum x2 -> x0, blocking collectives: 63.1 us -> none  [the longest x1 41.1 us: local(): lax.psum((lowering_grad, scaling_grad, centering_grad, rescaling_grad, re...]
    dot_general x12 -> x0, matrix products: 52.2 us -> none  [the longest x1 9.36 us: local(): jnp.einsum('rk,rd->kd', channel_low, out_low, preferred_element_type=jnp....]
    unnamed x74 -> x7, local copies, waits for them, and re-layouts: 41.2 us -> 12.1 us
    reduce_sum x12 -> x0, other arithmetic: 9.25 us -> none  [the longest x4 2.72 us: layer_norm(): return centre * lax.rsqrt(spread + 1e-06) * scale_vec + shift_vec]
  transfers between devices with their start and end apart: 7 -> 0, of which waited for: 4 -> 0; matrix products, arithmetic and copies ran while one was open for 17% -> 0% of each run, Pallas kernels for 0% -> 0%
where the time goes in v1:
time: 133 us; the launch traced here: 132 us
  Pallas kernels  107 us (80%)
  local copies, waits for them, and re-layouts  21.8 us (16%)
  between operations  1.33 us (1%)
    pallas_call x1, Pallas kernels, local(): pl.pallas_call(functools.partial(kernel, z), out_shape=(S((PT, images, D)...  107 us
    unnamed x7, local copies, waits for them, and re-layouts  12.1 us
    broadcast_in_dim x7, local copies, waits for them, and re-layouts, line(): return jnp.pad(v.astype(F32), (0, D - v.shape[0]))[None]  3.43 us

profile of v1, /device:TPU:0, one launch (start us, length us, event | category | flops | bytes accessed | tf_op | source)
XLA Modules:
  0.0 132.0 jit_solution(12114439870717503276)
XLA Ops:
  0.7 0.7 reshape.33
  1.4 0.7 pad_convert_fusion.2
  2.0 0.1 tile.10
  2.1 0.7 pad_convert_fusion.1
  2.8 0.7 reshape.34
  3.5 0.7 reshape.35
  4.2 0.7 reshape.36
  4.9 0.7 reshape.37
  5.5 0.7 reshape.38
  6.2 1.3 concatenate.3.prm
  7.5 1.5 %copy.29.ex = bf16[196,96]{1,0:T(8,128)(2,1)} copy(bf16[196,96]{0,1:T(8,128)(2,1)} %param.17) | data formatting | bytes 75264 | tf_op args[2]
  9.7 107.5 %shard_map.254 = (bf16[49,8,768]{2,1,0:T(8,128)(2,1)}, bf16[49,8,768]{2,1,0:T(8,128)(2,1)}, f32[196,96]{1,0:T(8,128)}, f32[8,96]{1,0:T(8,128)}, f32[96,196]{1,0:...) custom-call(s32[1]{0:T(128)S(6)} %copy.36.cnt, bf16[49,8,768]{2,1,0:T(8,128)(2,1)} %x.9, ...), custom_call_target="tpu_custom_call" | custom-call | tf_op jit(solution)/shard_map/pallas_call | solution.py:546
  117.2 1.3 dynamic-slice_bitcast_fusion
  118.5 1.3 dynamic-slice_bitcast_fusion.1
  119.7 1.7 %slice_reduce_fusion = (f32[768]{0:T(1024)}, f32[768]{0:T(1024)}, f32[768]{0:T(1024)}, f32[768]{0:T(1024)}, f32[768]{0:T(1024)}) fusion(f32[16,768]{1,0:T(8,128)} %get-tuple-element.27), kind=kLoop, calls=%fused_computation.1 | loop fusion | bytes 30720 | tf_op jit(solution)/shard_map/slice | solution.py:569
  121.4 1.9 %copy.31 = f32[768,96]{0,1:T(8,128)} copy(f32[768,96]{1,0:T(8,128)} %get-tuple-element.40) | data formatting | bytes 589824
  123.3 1.6 %copy.30 = f32[196,96]{0,1:T(8,128)} copy(f32[196,96]{1,0:T(8,128)} %get-tuple-element.32) | data formatting | bytes 150528
  124.9 1.9 %copy.37 = bf16[49,8,768]{2,1,0:T(8,128)(2,1)} copy(bf16[49,8,768]{2,1,0:T(8,128)(2,1)} %get-tuple-element.65) | data formatting | bytes 1204224
  126.8 1.9 %copy.38 = bf16[49,8,768]{2,1,0:T(8,128)(2,1)} copy(bf16[49,8,768]{2,1,0:T(8,128)(2,1)} %get-tuple-element.66) | data formatting | bytes 1204224
  128.7 1.5 %copy.39 = f32[96,196]{1,0:T(8,128)} copy(f32[96,196]{1,0:T(8,128)} %get-tuple-element.69) | data formatting | bytes 150528
  130.3 1.7 %copy.40 = f32[96,768]{1,0:T(8,128)} copy(f32[96,768]{1,0:T(8,128)} %get-tuple-element.77) | data formatting | bytes 589824
  (6 shorter events, 0.0 us)

commit v2 on v1

v2 whole, which is shorter than its diff:
```python
import functools

import jax
import jax.numpy as jnp
from jax import lax
from jax.experimental import pallas as pl
from jax.experimental.pallas import tpu as pltpu
from jax.sharding import PartitionSpec as P

MESH = pl.DeviceIdType.MESH
F32 = jnp.float32
BF16 = jnp.bfloat16
EPS = 1e-6
LANES = 128


def dot(a, b, ca, cb):
    return lax.dot_general(a, b, (((ca,), (cb,)), ((), ())), preferred_element_type=F32)


def dot_exact(a, b, ca, cb):
    return lax.dot_general(
        a, b, (((ca,), (cb,)), ((), ())), precision=lax.Precision.HIGHEST, preferred_element_type=F32
    )


def gelu_parts(v):
    c = 0.7978845608028654
    v2 = v * v
    t = jnp.tanh(c * v * (1.0 + 0.044715 * v2))
    half = 0.5 + 0.5 * t
    act = v * half
    slope = half + (0.5 * c) * v * (1.0 - t * t) * (1.0 + (3.0 * 0.044715) * v2)
    return act, slope


def norm_stats(v):
    cen = v - jnp.mean(v, axis=-1, keepdims=True)
    rs = lax.rsqrt(jnp.mean(cen * cen, axis=-1, keepdims=True) + EPS)
    return cen * rs, rs


def norm_back(grad, xhat, rs, gain):
    g = grad * gain
    return rs * (g - jnp.mean(g, axis=-1, keepdims=True) - xhat * jnp.mean(g * xhat, axis=-1, keepdims=True))


def pick_matrix(T, PT, PP):
    row = lax.broadcasted_iota(jnp.int32, (PT * T, PP * T), 0)
    col = lax.broadcasted_iota(jnp.int32, (PT * T, PP * T), 1)
    pick = jnp.zeros((PT * T, PP * T), F32)
    for t in range(T):
        inside = (col >= PP * t) & (col < PP * t + PT) & (row - PT * t == col - PP * t)
        pick = pick + jnp.where(inside, 1.0, 0.0)
    return pick


class Sizes:
    pass


ORDER = ((1, 1, 1), (1, 0, 1), (0, 1, 1), (0, 0, 1), (1, 1, 0), (1, 0, 0), (0, 1, 0), (0, 0, 0))


def layer_kernel(
    z,
    cnt, x, ct_hbm, ex, co, uplift, offset, scal, cent, resc, rece, lowr, rais, w1_hbm, w2_hbm,
    ro, ro2, fin, ecf, vec,
    ct, w1, w2, xs, sb, rb, et, cc, nb16, tp, ta, mixed, nr, ol, yacc, gacc, mgrad, bias, so, so2,
    gs, r1, rxp, ryp, rap, rbp, ryq, raq, rxq, rbq, rar, ryr, rxr, rbr,
    vv, vr, ec, ecr, es, er, tg16,
    lsem, a_s, a_r, w_s, w_r, c_s, c_r, xp_s, xp_r, yp_s, yp_r, ap_s, ap_r, bp_s, bp_r,
    yq_s, yq_r, aq_s, aq_r, xq_s, xq_r, bq_s, bq_r, ar_s, ar_r, yr_s, yr_r, xr_s, xr_r, br_s, br_r,
    o_s, o_r, v_s, v_r, e_s, e_r,
):
    D, PT, PP, R, HB, HC, T, NDP = z.D, z.PT, z.PP, z.R, z.HB, z.HC, z.T, z.NDP
    DSL, DS = z.DSL, z.DSL * T
    PL = PP * T
    half_r = R // 2
    dp = lax.axis_index("dp")
    te = lax.axis_index("tensor")
    di = lax.rem(dp, NDP)
    mc = lax.rem(te, 2)
    mx = te // 2
    my = lax.rem(di, 2)
    mz = di // 2

    def tpeer(o):
        if o == 1:
            return te + 1 - 2 * mc
        if o == 2:
            return lax.rem(te + 2, 4)
        return 3 - te

    core_dev = (dp, tpeer(1))
    x_dev = (dp, tpeer(2))
    y_dev = (dp + 1 - 2 * my, te)

    a_dev = (dp + 2 - 4 * lax.rem(mz, 2), te)
    b_dev = (dp - di + lax.rem(di + 4, NDP), te)
    ma, mb = lax.rem(mz, 2), mz // 2

    def rc(src, dst, ss, rs, dev):
        return pltpu.make_async_remote_copy(
            src_ref=src, dst_ref=dst, send_sem=ss, recv_sem=rs, device_id=dev, device_id_type=MESH
        )

    sent = []

    def send(copy):
        copy.start()
        sent.append(copy)

    lc_ct = pltpu.make_async_copy(ct_hbm, ct, lsem.at[0])
    lc_w1 = pltpu.make_async_copy(w1_hbm, w1, lsem.at[1])
    lc_w2 = pltpu.make_async_copy(w2_hbm, w2, lsem.at[2])
    lc_ct.start()

    peers = [(dp, tpeer(o)) for o in (1, 2, 3)] + [y_dev, a_dev, b_dev]
    bar = pltpu.get_barrier_semaphore()
    for dev in peers:
        pl.semaphore_signal(bar, inc=1, device_id=dev, device_id_type=MESH)

    def spread(src, k):
        for c in range(D // LANES):
            lanes = slice(c * LANES, (c + 1) * LANES)
            xs[c * PP * 8 : c * PP * 8 + PT * 8, :] = src[:, :, lanes].astype(F32).reshape(PT * 8, LANES)
            for j in range(T):
                for b in range(2):
                    sb[k, j, b, :, lanes] = xs[pl.ds(c * PP * 8 + 2 * j + b, PP, stride=8), :].astype(BF16)

    def a2a(k, o, b):
        j = tpeer(o)
        return rc(sb.at[k, j, b], rb.at[k, te, b], a_s.at[k, o - 1, b], a_r.at[k, o - 1, b], (dp, j))

    def a2a_in(k, o, b):
        j = tpeer(o)
        return rc(sb.at[k, j, b], rb.at[k, j, b], a_s.at[k, o - 1, b], a_r.at[k, o - 1, b], (dp, j))

    for c in range(D // LANES):
        xs[c * PP * 8 + PT * 8 : (c + 1) * PP * 8, :] = jnp.zeros((PP * 8 - PT * 8, LANES), F32)
    spread(x, 0)

    pick = pick_matrix(T, PT, PP)
    pick16 = pick.astype(BF16)
    col1 = lax.broadcasted_iota(jnp.int32, (1, PL), 1)
    pad_one = jnp.where(col1 == PT, 1.0, 0.0)
    uplift_col = dot_exact(uplift[...].astype(F32).reshape(1, DSL), pad_one, 0, 0)
    et[te, 0] = (dot(ex[...], pick16, 1, 0) + uplift_col).astype(BF16)
    et[te, 1] = dot(co[...], pick16, 1, 0).astype(BF16)
    off_line = offset[...].astype(F32).reshape(1, PT)
    own_cols = (lax.broadcasted_iota(jnp.int32, (PT, PL), 1) - PP * te) == lax.broadcasted_iota(
        jnp.int32, (PT, PL), 0
    )
    off_row = dot(off_line.astype(BF16), jnp.where(own_cols, 1.0, 0.0).astype(BF16), 1, 0)
    cc[te] = jnp.broadcast_to(off_row, (8, PL))

    pl.semaphore_wait(bar, len(peers))

    def wcopies(t, slot, dev):
        return [
            rc(et.at[t], et.at[t], w_s.at[0, slot], w_r.at[0, slot], dev),
            rc(cc.at[t], cc.at[t], w_s.at[1, slot], w_r.at[1, slot], dev),
        ]

    for o in (2, 3, 1):
        send(a2a(0, o, 0))
    for c in wcopies(te, 1, x_dev) + wcopies(te, 0, core_dev):
        send(c)
    for o in (2, 3, 1):
        send(a2a(0, o, 1))
    for b in range(2):
        rb[0, te, b] = sb[0, te, b]

    lc_ct.wait()
    lc_w1.start()
    lc_w2.start()
    spread(ct, 1)
    for b in range(2):
        for o in (2, 3, 1):
            send(a2a(1, o, b))
    for b in range(2):
        rb[1, te, b] = sb[1, te, b]

    for c in wcopies(tpeer(2), 1, x_dev):
        c.wait_recv()
    for c in wcopies(tpeer(2), 2, core_dev):
        send(c)
    bias_line = rais[...].astype(F32).reshape(1, HB * NDP)
    for d in range(NDP):
        bias[d : d + 1, :] = bias_line[:, d * HB : (d + 1) * HB]
    scaling, centering = scal[...].astype(F32).reshape(1, D), cent[...].astype(F32).reshape(1, D)
    rescaling, recentering = resc[...].astype(F32).reshape(1, D), rece[...].astype(F32).reshape(1, D)
    lowering = lowr[...].astype(F32).reshape(1, D)
    for c in wcopies(tpeer(1), 0, core_dev) + wcopies(tpeer(3), 2, core_dev):
        c.wait_recv()

    e_t = et[:, 0].reshape(DS, PL)
    c_t = et[:, 1].reshape(DS, PL)
    zero_pad = lax.broadcasted_iota(jnp.int32, (DS, PL), 1) == PT
    e_clean = jnp.where(zero_pad, 0.0, e_t.astype(F32)).astype(BF16)
    off_full = (cc[0] + cc[1]) + (cc[2] + cc[3])
    first8 = lax.broadcasted_iota(jnp.int32, (8, PL), 0) == 0
    off_row8 = jnp.where(first8, off_full, 0.0).astype(BF16)
    ones_row = lax.broadcasted_iota(jnp.int32, (half_r, 1), 0) == PT
    ones8 = jnp.where(lax.broadcasted_iota(jnp.int32, (8, D), 0) == 0, 1.0, 0.0).astype(BF16)

    def image_rows(k, b):
        return jnp.concatenate([rb[k, t, b].astype(F32) for t in range(T)], axis=0)

    for b in range(2):
        for o in (1, 2, 3):
            a2a_in(0, o, b).wait_recv()
        sl = slice(b * half_r, (b + 1) * half_r)
        xb = image_rows(0, b)
        xhat, _ = norm_stats(xb)
        n = jnp.where(ones_row, 1.0, xhat * scaling + centering).astype(BF16)
        nb16[sl, :] = n
        pre = dot(e_t, n, 1, 0)
        tp[b] = pre
        act, _ = gelu_parts(pre)
        ta[b, 0:DS, :] = act.astype(BF16)
        ta[b, DS : DS + 8, :] = ones8
        mx_b = xb + dot(c_t, ta[b, 0:DS, :], 0, 0) + dot(off_row8, ones8, 0, 0)
        mixed[sl, :] = mx_b
        xh2, _ = norm_stats(mx_b)
        nr[sl, :] = (xh2 * rescaling + recentering).astype(BF16)

    low_sum = jnp.zeros((1, D), F32)
    for b in range(2):
        for o in (1, 2, 3):
            a2a_in(1, o, b).wait_recv()
        sl = slice(b * half_r, (b + 1) * half_r)
        keep = jnp.where(2 * te + b < cnt[0], 1.0, 0.0)
        og = image_rows(1, b) * keep
        ol[sl, :] = og.astype(BF16)
        low_sum = low_sum + jnp.sum(og, axis=0, keepdims=True)
    vv[0] = jnp.zeros(vv.shape[1:], F32)
    vv[0, 4:5, :] = low_sum
    yacc[...] = jnp.zeros(yacc.shape, F32)
    gacc[...] = jnp.zeros(gacc.shape, F32)
    lc_w1.wait()
    lc_w2.wait()

    PR, QR, RR = pl.ds(0, z.P), pl.ds(z.P, z.Q), pl.ds(z.P + z.Q, HC - z.P - z.Q)
    pos = {o: i for i, o in enumerate(ORDER)}

    def add_into(dst, src):
        dst[...] = (dst[...].astype(F32) + src[...].astype(F32)).astype(BF16)

    def core_copy(i):
        return rc(gs.at[i, 1 - mc], r1.at[i], c_s.at[i], c_r.at[i], core_dev)

    def xp_copy(i):
        return rc(gs.at[i, mc, 1 - mx, :, PR], rxp.at[i], xp_s.at[i], xp_r.at[i], x_dev)

    def yq_copy(i):
        return rc(gs.at[i, mc, :, :, QR], ryq.at[i], yq_s.at[i], yq_r.at[i], y_dev)

    def ar_copy(i):
        return rc(gs.at[i, mc, :, :, RR], rar.at[i], ar_s.at[i], ar_r.at[i], a_dev)

    def after_core(i):
        core_copy(i).wait_recv()
        for xx in range(2):
            for g in range(2):
                add_into(gs.at[i, mc, xx, g], r1.at[i, xx, g])
        xp_copy(i).start()

    def among(i, bit):
        hit = jnp.int32(0)
        for k, o in enumerate(ORDER):
            if o[bit]:
                hit = hit + jnp.where(i == k, 1, 0)
        return hit

    def flip(m, bit):
        return m + bit - 2 * m * bit

    def begin(copy):
        copy.start()

    def add_rows(i, rows, src, both):
        for g in range(2):
            if both:
                for xx in range(2):
                    add_into(gs.at[i, mc, xx, g, rows], src.at[xx, g])
            else:
                add_into(gs.at[i, mc, mx, g, rows], src.at[g])

    def own(i, rows):
        return gs.at[i, mc, mx, :, rows]

    def oth(i, rows):
        return gs.at[i, mc, 1 - mx, :, rows]

    def yp_copy(da, db):
        k = 2 * da + db
        return rc(own(pos[1, da, db], PR), ryp.at[k], yp_s.at[k], yp_r.at[k], y_dev)

    def ap_copy(db):
        return rc(own(pos[0, 1, db], PR), rap.at[db], ap_s.at[db], ap_r.at[db], a_dev)

    bp_copy = rc(own(pos[0, 0, 1], PR), rbp, bp_s, bp_r, b_dev)

    def take_xp(o, send=send):
        xp_copy(pos[o]).wait_recv()
        add_rows(pos[o], PR, rxp.at[pos[o]], False)
        if o[0]:
            send(yp_copy(o[1], o[2]))

    def take_yp(da, db):
        yp_copy(da, db).wait_recv()
        add_rows(pos[0, da, db], PR, ryp.at[2 * da + db], False)
        if da:
            send(ap_copy(db))

    def take_ap(db):
        ap_copy(db).wait_recv()
        add_rows(pos[0, 0, db], PR, rap.at[db], False)
        if db:
            send(bp_copy)

    def aq_copy(db):
        return rc(gs.at[pos[0, 1, db], mc, :, :, QR], raq.at[db], aq_s.at[db], aq_r.at[db], a_dev)

    def xq_copy(db):
        return rc(oth(pos[0, 0, db], QR), rxq.at[db], xq_s.at[db], xq_r.at[db], x_dev)

    bq_copy = rc(own(pos[0, 0, 1], QR), rbq, bq_s, bq_r, b_dev)

    def take_yq(da, db, send=send):
        yq_copy(pos[1, da, db]).wait_recv()
        add_rows(pos[0, da, db], QR, ryq.at[pos[1, da, db]], True)
        if da:
            send(aq_copy(db))

    def take_aq(db):
        aq_copy(db).wait_recv()
        add_rows(pos[0, 0, db], QR, raq.at[db], True)
        send(xq_copy(db))

    def take_xq(db):
        xq_copy(db).wait_recv()
        add_rows(pos[0, 0, db], QR, rxq.at[db], False)
        if db:
            send(bq_copy)

    def yr_copy(db):
        return rc(gs.at[pos[1, 0, db], mc, :, :, RR], ryr.at[db], yr_s.at[db], yr_r.at[db], y_dev)

    def xr_copy(db):
        return rc(oth(pos[0, 0, db], RR), rxr.at[db], xr_s.at[db], xr_r.at[db], x_dev)

    br_copy = rc(own(pos[0, 0, 1], RR), rbr, br_s, br_r, b_dev)

    def take_ar(dy, db, send=send):
        ar_copy(pos[dy, 1, db]).wait_recv()
        add_rows(pos[dy, 0, db], RR, rar.at[pos[dy, 1, db]], True)
        if dy:
            send(yr_copy(db))

    def take_yr(db):
        yr_copy(db).wait_recv()
        add_rows(pos[0, 0, db], RR, ryr.at[db], True)
        send(xr_copy(db))

    def take_xr(db):
        xr_copy(db).wait_recv()
        add_rows(pos[0, 0, db], RR, rxr.at[db], False)
        if db:
            send(br_copy)

    def block(i, carry):
        d = flip(mb, among(i, 2)) * 4 + flip(ma, among(i, 1)) * 2 + flip(my, among(i, 0))
        cols = pl.ds(pl.multiple_of(d * HB, HB), HB)
        w1d = w1[:, cols]
        w2d = w2[cols, :]
        pre = dot(nr[...], w1d, 1, 0) + bias[pl.ds(d, 1), :]
        act, slope = gelu_parts(pre)
        act16 = act.astype(BF16)
        low16 = (slope * dot(ol[...], w2d, 1, 1)).astype(BF16)
        gn = dot(act16, ol[...], 0, 0)
        gb = dot(low16, nr[...], 0, 0)
        for t in range(T):
            rows = slice(t * HC, (t + 1) * HC)
            gs[i, t % 2, t // 2, 0] = gn[rows, :].astype(BF16)
            gs[i, t % 2, t // 2, 1] = gb[rows, :].astype(BF16)
        core_copy(i).start()
        yacc[...] += dot(act16, w2d, 1, 0)
        gacc[...] += dot(low16, w1d, 1, 1)
        vv[0, pl.ds(8 + d, 1), 0:HB] = jnp.sum(low16.astype(F32), axis=0, keepdims=True)

        @pl.when(i > 0)
        def _():
            after_core(i - 1)

            @pl.when(among(i - 1, 0) == 1)
            def _():
                yq_copy(i - 1).start()

            @pl.when(among(i - 1, 1) == 1)
            def _():
                ar_copy(i - 1).start()

        @pl.when(i == 5)
        def _():
            take_yq(1, 1, begin)
            take_ar(1, 1, begin)
            take_xp((1, 1, 1), begin)
            take_xp((1, 0, 1), begin)

        @pl.when(i == 6)
        def _():
            take_yq(0, 1, begin)
            take_ar(0, 1, begin)
            take_xp((0, 1, 1), begin)
            take_xp((0, 0, 1), begin)

        return carry

    lax.fori_loop(0, NDP, block, 0)
    after_core(NDP - 1)
    sent.extend([aq_copy(1), yr_copy(1), yp_copy(1, 1), yp_copy(0, 1)])
    sent.extend([core_copy(i) for i in range(NDP)] + [xp_copy(i) for i in range(NDP)])
    sent.extend([yq_copy(i) for i, o in enumerate(ORDER) if o[0]] + [ar_copy(i) for i, o in enumerate(ORDER) if o[1]])

    def ocopy(k, o, b):
        src, dst = (so, ro) if k == 0 else (so2, ro2)
        j = tpeer(o)
        return rc(src.at[j, b], dst.at[te, b], o_s.at[k, o - 1, b], o_r.at[k, o - 1, b], (dp, j))

    def ocopy_in(k, o, b):
        src, dst = (so, ro) if k == 0 else (so2, ro2)
        j = tpeer(o)
        return rc(src.at[j, b], dst.at[j, b], o_s.at[k, o - 1, b], o_r.at[k, o - 1, b], (dp, j))

    lc_o = [pltpu.make_async_copy(s.at[te], r.at[te], lsem.at[3 + k]) for k, (s, r) in enumerate(((so, ro), (so2, ro2)))]

    def out_image(b):
        keep = jnp.where(2 * te + b < cnt[0], 1.0, 0.0)
        for t in range(T):
            r0 = b * half_r + t * PP
            sl = slice(r0, r0 + PP)
            so[t, b] = ((mixed[sl, :] + yacc[sl, :] + lowering) * keep).astype(BF16)
        for o in (2, 3, 1):
            send(ocopy(0, o, b))

    take_aq(1)
    take_yr(1)
    out_image(0)

    resc_sum = jnp.zeros((1, D), F32)
    rece_sum = jnp.zeros((1, D), F32)
    for b in range(2):
        sl = slice(b * half_r, (b + 1) * half_r)
        xh2, rs2 = norm_stats(mixed[sl, :])
        gr = gacc[sl, :]
        resc_sum = resc_sum + jnp.sum(gr * xh2, axis=0, keepdims=True)
        rece_sum = rece_sum + jnp.sum(gr, axis=0, keepdims=True)
        mgrad[sl, :] = ol[sl, :].astype(F32) + norm_back(gr, xh2, rs2, rescaling)
    vv[0, 2:3, :] = resc_sum
    vv[0, 3:4, :] = rece_sum

    take_yq(1, 0)
    take_ar(1, 0)
    take_xp((1, 1, 0))
    take_xp((1, 0, 0))

    eg_sum = jnp.zeros((DS, PL), F32)
    cg_sum = jnp.zeros((DS + 8, PL), F32)
    for b in range(2):
        sl = slice(b * half_r, (b + 1) * half_r)
        ml = mgrad[sl, :].astype(BF16)
        _, slope = gelu_parts(tp[b])
        tg = (slope * dot(c_t, ml, 1, 0)).astype(BF16)
        tg16[b] = tg
        cg_sum = cg_sum + dot(ta[b], ml, 1, 1)
        eg_sum = eg_sum + dot(tg, nb16[sl, :], 1, 1)
    vv[0, 5:6, 0:PL] = cg_sum[DS : DS + 1, :]
    for t in range(T):
        ec[t % 2, t // 2, 0] = eg_sum[t * DSL : (t + 1) * DSL, :]
        ec[t % 2, t // 2, 1] = cg_sum[t * DSL : (t + 1) * DSL, :]

    def v_copy(s, dev):
        return rc(vv.at[s], vr.at[s], v_s.at[s], v_r.at[s], dev)

    def e_copy(s, dev):
        return rc(es.at[s], er.at[s], e_s.at[s + 1], e_r.at[s + 1], dev)

    def v_next(s, dev, nxt):
        v_copy(s, dev).wait_recv()
        vv[s + 1] = vv[s] + vr[s]
        if nxt is not None:
            send(v_copy(s + 1, nxt))

    def e_next(s, dev, nxt):
        e_copy(s, dev).wait_recv()
        if s == 0:
            tot = ec[mc, mx] + ecr[mx] + er[s].astype(F32)
        else:
            tot = es[s].astype(F32) + er[s].astype(F32)
        if nxt is None:
            ecf[...] = tot
        else:
            es[s + 1] = tot.astype(BF16)
            send(e_copy(s + 1, nxt))

    e_core = rc(ec.at[1 - mc], ecr, e_s.at[0], e_r.at[0], core_dev)
    send(e_core)

    def first_back(b):
        nback = dot(e_clean, tg16[b], 0, 0)
        xhat, rs1 = norm_stats(image_rows(0, b))
        sl = slice(b * half_r, (b + 1) * half_r)
        grad = (mgrad[sl, :] + norm_back(nback, xhat, rs1, scaling)).astype(BF16)
        for t in range(T):
            so2[t, b] = grad[t * PP : (t + 1) * PP, :]
        return jnp.sum(nback * xhat, axis=0, keepdims=True), jnp.sum(nback, axis=0, keepdims=True)

    scal0, cent0 = first_back(0)
    e_core.wait_recv()
    es[0] = (ec[mc, 1 - mx] + ecr[1 - mx]).astype(BF16)
    send(e_copy(0, x_dev))
    scal1, cent1 = first_back(1)
    vv[0, 0:1, :] = scal0 + scal1
    vv[0, 1:2, :] = cent0 + cent1
    send(v_copy(0, core_dev))
    take_yp(1, 1)
    take_yp(0, 1)
    take_yq(0, 0)
    take_ar(0, 0)
    take_xp((0, 1, 0))
    take_xp((0, 0, 0))
    v_next(0, core_dev, x_dev)
    take_xq(1)
    take_xr(1)
    out_image(1)
    lc_o[0].start()
    take_aq(0)
    take_yr(0)
    for b in range(2):
        for o in (2, 3, 1):
            send(ocopy(1, o, b))
    lc_o[1].start()
    e_next(0, x_dev, y_dev)
    v_next(1, x_dev, y_dev)
    take_ap(1)
    take_yp(1, 0)
    take_yp(0, 0)
    e_next(1, y_dev, a_dev)
    v_next(2, y_dev, a_dev)
    take_xq(0)
    take_xr(0)
    take_ap(0)
    e_next(2, a_dev, b_dev)
    v_next(3, a_dev, b_dev)

    def last(copy, rows, buf):
        copy.wait_recv()
        for g in range(2):
            fin[g, rows, :] = gs[NDP - 1, mc, mx, g, rows, :].astype(F32) + buf[g].astype(F32)

    last(bq_copy, QR, rbq)
    last(br_copy, RR, rbr)
    last(bp_copy, PR, rbp)
    e_next(3, b_dev, None)
    v_next(4, b_dev, None)
    vec[...] = vv[5]
    for k in range(2):
        for o in (1, 2, 3):
            for b in range(2):
                ocopy_in(k, o, b).wait_recv()
        lc_o[k].wait()

    for c in sent:
        c.wait_send()


def finish_kernel(
    z, ro_h, ro2_h, fin_h, ecf_h, vec_h, lo, ig, eg, up, cg, off, v0, v1, v2, v3, bg, rg, ng, v4,
    xs, ro, ro2, ecf, vec, sem,
):
    D, PT, PP, HB, HC, T, NDP, DSL = z.D, z.PT, z.PP, z.HB, z.HC, z.T, z.NDP, z.DSL
    te = lax.axis_index("tensor")
    di = lax.rem(lax.axis_index("dp"), NDP)
    pairs = ((ro_h, ro), (ro2_h, ro2), (ecf_h, ecf), (vec_h, vec), (fin_h.at[0], ng), (fin_h.at[1], bg))
    loads = [pltpu.make_async_copy(src, dst, sem.at[k]) for k, (src, dst) in enumerate(pairs)]
    for c in loads:
        c.start()
    for k, (src, dst) in enumerate(((ro, lo), (ro2, ig))):
        loads[k].wait()
        for c in range(D // LANES):
            lanes = slice(c * LANES, (c + 1) * LANES)
            for j in range(T):
                for b in range(2):
                    xs[pl.ds(c * PP * 8 + 2 * j + b, PP, stride=8), :] = src[j, b, :, lanes].astype(F32)
            dst[:, :, lanes] = xs[c * PP * 8 : c * PP * 8 + PT * 8, :].reshape(PT, 8, LANES).astype(BF16)
    for c in loads[2:]:
        c.wait()
    pick = pick_matrix(T, PT, PP)
    eg[...] = dot_exact(ecf[0], pick, 1, 1)
    cg[...] = dot_exact(ecf[1], pick, 1, 1)
    row8 = lax.broadcasted_iota(jnp.int32, (8, PP * T), 1)
    up[...] = dot_exact(jnp.where(row8 == PT, 1.0, 0.0), ecf[0], 1, 1)[0:1, :].reshape(DSL)
    for ref, r in ((v0, 0), (v1, 1), (v2, 2), (v3, 3), (v4, 4)):
        ref[...] = vec[r : r + 1, :].reshape(D)
    off_row = vec[5:6, :]
    rg_row = vec[pl.ds(8 + di, 1), :]
    off_own = jnp.zeros((1, PT), F32)
    rg_own = jnp.zeros((1, HC), F32)
    for t in range(T):
        off_own = off_own + jnp.where(te == t, off_row[:, t * PP : t * PP + PT], 0.0)
        rg_own = rg_own + jnp.where(te == t, rg_row[:, t * HC : (t + 1) * HC], 0.0)
    off[...] = off_own.reshape(PT)
    rg[...] = rg_own.reshape(HC)


def local(
    layer_input, image_counts, expand, uplift, contract, offset, scaling, centering,
    rescaling, recentering, broaden, raising, narrow, lowering, cotangent, *, mesh,
):
    z = Sizes()
    z.PT, images, z.D = layer_input.shape
    z.T, z.NDP = mesh.shape["tensor"], 8
    outer = mesh.shape["dp"] // z.NDP
    z.PP = -(-(z.PT + 1) // 8) * 8
    z.R = 2 * z.T * z.PP
    hidden = broaden.shape[1]
    if outer > 1:
        split = (outer, z.NDP, z.T, hidden // (outer * z.NDP * z.T))
        broaden = broaden.reshape(-1, *split).transpose(0, 2, 3, 1, 4).reshape(-1, hidden)
        raising = raising.reshape(split).transpose(1, 2, 0, 3).reshape(hidden)
        narrow = narrow.reshape(*split, -1).transpose(1, 2, 0, 3, 4).reshape(hidden, -1)
    z.HB = hidden // z.NDP
    z.HC = z.HB // z.T
    z.DSL = expand.shape[1]
    D, T, NDP, PP, PT, R, HB, HC, DSL = z.D, z.T, z.NDP, z.PP, z.PT, z.R, z.HB, z.HC, z.DSL
    DS, PL = DSL * T, PP * T

    vm = pl.BlockSpec(memory_space=pltpu.VMEM)
    anys = pl.BlockSpec(memory_space=pl.ANY)
    dma = pltpu.SemaphoreType.DMA
    V = pltpu.VMEM
    S = jax.ShapeDtypeStruct
    z.P, z.Q = HC // 3, HC // 3
    P_, Q_, R_ = z.P, z.Q, HC - z.P - z.Q
    sems = []
    for shape in (
        (2, 3, 2), (2, 3), (NDP,), (NDP,), (4,), (2,), (), (NDP,), (2,), (2,), (), (NDP,), (2,), (2,), (),
        (2, 3, 2), (5,), (5,),
    ):
        sems += [dma(shape), dma(shape)]
    scratch = [
        V((PT, 8, D), BF16), V(broaden.shape, BF16), V(narrow.shape, BF16), V((D // LANES * PP * 8, LANES), F32),
        V((2, T, 2, PP, D), BF16), V((2, T, 2, PP, D), BF16), V((T, 2, DSL, PL), BF16), V((T, 8, PL), F32),
        V((R, D), BF16), V((2, DS, D), F32), V((2, DS + 8, D), BF16), V((R, D), F32), V((R, D), BF16), V((R, D), BF16),
        V((R, D), F32), V((R, D), F32), V((R, D), F32), V((NDP, HB), F32), V((T, 2, PP, D), BF16), V((T, 2, PP, D), BF16),
        V((NDP, 2, 2, 2, HC, D), BF16), V((NDP, 2, 2, HC, D), BF16),
        V((NDP, 2, P_, D), BF16), V((4, 2, P_, D), BF16), V((2, 2, P_, D), BF16), V((2, P_, D), BF16),
        V((NDP, 2, 2, Q_, D), BF16), V((2, 2, 2, Q_, D), BF16), V((2, 2, Q_, D), BF16), V((2, Q_, D), BF16),
        V((NDP, 2, 2, R_, D), BF16), V((2, 2, 2, R_, D), BF16), V((2, 2, R_, D), BF16), V((2, R_, D), BF16),
        V((6, 16, D), F32), V((5, 16, D), F32), V((2, 2, 2, DSL, PL), F32), V((2, 2, DSL, PL), F32),
        V((4, 2, DSL, PL), BF16), V((4, 2, DSL, PL), BF16), V((2, DS, D), BF16),
        dma((5,)),
    ] + sems
    mid = pl.pallas_call(
        functools.partial(layer_kernel, z),
        out_shape=(
            S((T, 2, PP, D), BF16), S((T, 2, PP, D), BF16), S((2, HC, D), F32), S((2, DSL, PL), F32), S((16, D), F32),
        ),
        in_specs=[pl.BlockSpec(memory_space=pltpu.SMEM), vm, anys] + [vm] * 10 + [anys, anys],
        out_specs=(anys, anys, vm, vm, vm),
        scratch_shapes=scratch,
        compiler_params=pltpu.CompilerParams(
            collective_id=0, has_side_effects=True, vmem_limit_bytes=60 * 1024 * 1024
        ),
    )(
        image_counts, layer_input, cotangent, expand.T, contract, uplift, offset, scaling, centering,
        rescaling, recentering, lowering, raising, broaden, narrow,
    )
    res = pl.pallas_call(
        functools.partial(finish_kernel, z),
        out_shape=(
            S((PT, images, D), BF16), S((PT, images, D), BF16), S((DSL, PT * T), F32), S((DSL,), F32),
            S((DSL, PT * T), F32), S((PT,), F32), S((D,), F32), S((D,), F32), S((D,), F32), S((D,), F32),
            S((HC, D), F32), S((HC,), F32), S((HC, D), F32), S((D,), F32),
        ),
        in_specs=[anys] * 5,
        out_specs=(vm,) * 14,
        scratch_shapes=[
            V((D // LANES * PP * 8, LANES), F32), V((T, 2, PP, D), BF16), V((T, 2, PP, D), BF16), V((2, DSL, PL), F32),
            V((16, D), F32), dma((6,)),
        ],
        compiler_params=pltpu.CompilerParams(vmem_limit_bytes=60 * 1024 * 1024),
    )(*mid)
    lo, ig, eg, up, cg, off, v0, v1, v2, v3, bg, rg, ng, v4 = res
    if outer > 1:
        same = [[o * NDP + i for o in range(outer)] for i in range(NDP)]
        eg, up, cg, off, v0, v1, v2, v3, v4 = lax.psum(
            (eg, up, cg, off, v0, v1, v2, v3, v4), "dp", axis_index_groups=same
        )
        bg, ng, rg = (
            lax.psum_scatter(v, "dp", scatter_dimension=0, axis_index_groups=same, tiled=True) for v in (bg, ng, rg)
        )
    return lo, ig, eg.T, up, cg, off, v0, v1, v2, v3, bg.T, rg, ng, v4


def solution(mesh):
    rows = P("tensor", "dp", None)
    both = ("dp", "tensor")
    in_specs = (
        rows, P("dp"), P(None, "tensor"), P("tensor"), P("tensor", None), P("tensor"),
        P(), P(), P(), P(), P(), P(), P(), P(), rows,
    )
    out_specs = (
        rows, rows, P(None, "tensor"), P("tensor"), P("tensor", None), P("tensor"),
        P(), P(), P(), P(), P(None, both), P(both), P(both, None), P(),
    )
    return jax.shard_map(
        functools.partial(local, mesh=mesh), mesh=mesh, in_specs=in_specs, out_specs=out_specs, check_vma=False
    )
```

time: 133 us -> 91.7 us (0.69)
  local copies, waits for them, and re-layouts: 21.8 us -> 0 us
  Pallas kernels: 107 us -> 90.1 us
    pallas_call x1 -> x2, Pallas kernels: 107 us -> 90.1 us  [the longest x1 86.6 us: local(): pl.pallas_call(functools.partial(layer_kernel, z), out_shape=(S((T, 2, PP...]
    unnamed x7 -> x0, local copies, waits for them, and re-layouts: 12.1 us -> none
    broadcast_in_dim x8 -> x0, local copies, waits for them, and re-layouts: 3.44 us -> none  [the longest x7 3.43 us: line(): return jnp.pad(v.astype(F32), (0, D - v.shape[0]))[None]]
    squeeze x2 -> x0, local copies, waits for them, and re-layouts: 2.58 us -> none  [the longest x1 1.3 us: local(): rg = lax.dynamic_slice(vec, (8 + dp, te * HC), (1, HC))[0]]
    slice x1 -> x0, local copies, waits for them, and re-layouts: 1.66 us -> none  [local(): vec[4]]
where the time goes in v2:
time: 91.7 us; the launch traced here: 91.6 us
  Pallas kernels  90.1 us (98%)
  between operations  1.46 us (2%)
    pallas_call x1, Pallas kernels, local(): pl.pallas_call(functools.partial(layer_kernel, z), out_shape=(S((T, 2, PP...  86.6 us
    pallas_call x1, Pallas kernels, local(): pl.pallas_call(functools.partial(finish_kernel, z), out_shape=(S((PT, ima...  3.45 us

profile of v2, /device:TPU:0, one launch (start us, length us, event | category | flops | bytes accessed | tf_op | source)
XLA Modules:
  0.0 91.6 jit_solution(1347536285809607666)
XLA Ops:
  1.3 86.6 %shard_map.254 = (bf16[4,2,56,768]{3,2,1,0:T(8,128)(2,1)}, bf16[4,2,56,768]{3,2,1,0:T(8,128)(2,1)}, f32[2,96,768]{2,1,0:T(8,128)}, f32[2,96,224]{2,1,0:T(8,128)}, f32[16,768]{1,0:T(8,128)}) custom-call(s32[1]{0:T(128)S(6)} %copy.29.cnt, bf16[49,8,768]{2,1,0:T(8,128)(2,1)} %x.1, bf16[49,8,768]{2,1,0:T(8,128)(2,1)} %ct_hbm.1, bf16[96,196]{1,0:T(8,128)(2,1)} %bitcast.3, ...), custom_call_target="tpu_custom_call" | custom-call | tf_op jit(solution)/shard_map/pallas_call | solution.py:667
  88.0 3.5 %shard_map.255 = (bf16[49,8,768]{2,1,0:T(8,128)(2,1)}, bf16[49,8,768]{2,1,0:T(8,128)(2,1)}, f32[96,196]{1,0:T(8,128)}, f32[96]{0:T(128)}, f32[96,196]{1,0:T(8,12...) custom-call(bf16[4,2,56,768]{3,2,1,0:T(8,128)(2,1)} %get-tuple-eleme, ...), custom_call_target="tpu_custom_call" | custom-call | tf_op jit(solution)/shard_map/pallas_call | solution.py:682

commit v3 on v2

v3 whole, which is shorter than its diff:
```python
import functools

import jax
import jax.numpy as jnp
from jax import lax
from jax.experimental import pallas as pl
from jax.experimental.pallas import tpu as pltpu
from jax.sharding import PartitionSpec as P

MESH = pl.DeviceIdType.MESH
F32 = jnp.float32
BF16 = jnp.bfloat16
EPS = 1e-6
LANES = 128


def dot(a, b, ca, cb):
    return lax.dot_general(a, b, (((ca,), (cb,)), ((), ())), preferred_element_type=F32)


def dot_exact(a, b, ca, cb):
    return lax.dot_general(
        a, b, (((ca,), (cb,)), ((), ())), precision=lax.Precision.HIGHEST, preferred_element_type=F32
    )


def gelu_parts(v):
    c = 0.7978845608028654
    v2 = v * v
    t = jnp.tanh(c * v * (1.0 + 0.044715 * v2))
    half = 0.5 + 0.5 * t
    act = v * half
    slope = half + (0.5 * c) * v * (1.0 - t * t) * (1.0 + (3.0 * 0.044715) * v2)
    return act, slope


def norm_stats(v):
    cen = v - jnp.mean(v, axis=-1, keepdims=True)
    rs = lax.rsqrt(jnp.mean(cen * cen, axis=-1, keepdims=True) + EPS)
    return cen * rs, rs


def norm_back(grad, xhat, rs, gain):
    g = grad * gain
    return rs * (g - jnp.mean(g, axis=-1, keepdims=True) - xhat * jnp.mean(g * xhat, axis=-1, keepdims=True))


def pick_matrix(T, PT, PP):
    row = lax.broadcasted_iota(jnp.int32, (PT * T, PP * T), 0)
    col = lax.broadcasted_iota(jnp.int32, (PT * T, PP * T), 1)
    pick = jnp.zeros((PT * T, PP * T), F32)
    for t in range(T):
        inside = (col >= PP * t) & (col < PP * t + PT) & (row - PT * t == col - PP * t)
        pick = pick + jnp.where(inside, 1.0, 0.0)
    return pick


class Sizes:
    pass


ORDER = ((1, 1, 1), (0, 1, 1), (1, 0, 1), (0, 0, 1), (1, 1, 0), (0, 1, 0), (1, 0, 0), (0, 0, 0))

EARLY = (
    (1, (
        ("yq", 1, 1), ("ar", 1, 1),
    )),
)
LATE = (
    ("yq", 0, 1), ("ar", 0, 1), ("yr", 1), ("ln2",), ("xp", 1, 0, 1), ("tok",), ("xp", 0, 0, 1), ("xp", 1, 1, 1),
    ("xp", 0, 1, 0), ("f", 0), ("xp", 0, 1, 1), ("aq", 1), ("e", 0), ("lo", 0), ("yq", 1, 0), ("f", 1),
    ("xp", 1, 1, 0), ("xp", 0, 0, 0), ("xr", 1), ("xq", 1), ("ar", 0, 0), ("v", 0), ("e", 1), ("v", 1), ("ar", 1, 0),
    ("ig", 0), ("yp", 1, 1), ("e", 2), ("yq", 0, 0), ("aq", 0), ("yp", 0, 1), ("ap", 1), ("yp", 1, 0), ("v", 2),
    ("lo", 1), ("e", 3), ("v", 3), ("yr", 0), ("xp", 1, 0, 0), ("ig", 1), ("xq", 0), ("v", 4), ("yp", 0, 0),
    ("v", 5), ("ap", 0), ("xr", 0), ("e", 4),
)


def layer_kernel(
    z,
    cnt, x, ct_hbm, ex, co, uplift, offset, scal, cent, resc, rece, lowr, rais, w1_hbm, w2_hbm,
    ro, ro2, fin, ecf, vec,
    ct, w1, w2, xs, sb, rb, et, cc, nb16, tp, ta, mixed, nr, ol, yacc, gacc, mgrad, bias, so, so2, ext, act_s, low_s, sums,
    gs, r1, rxp, ryp, rap, rbp, ryq, raq, rxq, rbq, rar, ryr, rxr, rbr,
    vv, vr, ec, ecr, es, er, tg16,
    lsem, a_s, a_r, w_s, w_r, c_s, c_r, xp_s, xp_r, yp_s, yp_r, ap_s, ap_r, bp_s, bp_r,
    yq_s, yq_r, aq_s, aq_r, xq_s, xq_r, bq_s, bq_r, ar_s, ar_r, yr_s, yr_r, xr_s, xr_r, br_s, br_r,
    o_s, o_r, v_s, v_r, e_s, e_r,
):
    D, PT, PP, R, HB, HC, T, NDP = z.D, z.PT, z.PP, z.R, z.HB, z.HC, z.T, z.NDP
    DSL, DS = z.DSL, z.DSL * T
    PL = PP * T
    half_r = R // 2
    dp = lax.axis_index("dp")
    te = lax.axis_index("tensor")
    di = lax.rem(dp, NDP)
    mc = lax.rem(te, 2)
    mx = te // 2
    my = lax.rem(di, 2)
    mz = di // 2

    def tpeer(o):
        if o == 1:
            return te + 1 - 2 * mc
        if o == 2:
            return lax.rem(te + 2, 4)
        return 3 - te

    core_dev = (dp, tpeer(1))
    x_dev = (dp, tpeer(2))
    y_dev = (dp + 1 - 2 * my, te)

    a_dev = (dp + 2 - 4 * lax.rem(mz, 2), te)
    b_dev = (dp - di + lax.rem(di + 4, NDP), te)
    ma, mb = lax.rem(mz, 2), mz // 2

    def rc(src, dst, ss, rs, dev):
        return pltpu.make_async_remote_copy(
            src_ref=src, dst_ref=dst, send_sem=ss, recv_sem=rs, device_id=dev, device_id_type=MESH
        )

    sent = []

    def send(copy):
        copy.start()
        sent.append(copy)

    lc_ct = pltpu.make_async_copy(ct_hbm, ct, lsem.at[0])
    lc_w1 = pltpu.make_async_copy(w1_hbm, w1, lsem.at[1])
    lc_w2 = pltpu.make_async_copy(w2_hbm, w2, lsem.at[2])
    lc_ct.start()

    peers = [(dp, tpeer(o)) for o in (1, 2, 3)] + [y_dev, a_dev, b_dev]
    bar = pltpu.get_barrier_semaphore()
    for dev in peers:
        pl.semaphore_signal(bar, inc=1, device_id=dev, device_id_type=MESH)

    row8 = lax.broadcasted_iota(jnp.int32, (8, LANES), 0)
    PM = PT - PT % 8
    IMG = (slice(0, PM), slice(PP, PP + PM))
    IN = (pl.ds(0, PP), pl.ds(PP, PM))
    OUT = (pl.ds(0, PM), pl.ds(PM, PP))

    def spread(src, k):
        for c in range(D // LANES):
            lanes = slice(c * LANES, (c + 1) * LANES)
            base = c * PT * 8
            xs[base : base + PT * 8, :] = src[:, :, lanes].astype(F32).reshape(PT * 8, LANES)
            tail = xs[base + PM * 8 : base + PT * 8, :]
            for j in range(T):
                for b in range(2):
                    sb[k, j, IMG[b], lanes] = xs[pl.ds(base + 2 * j + b, PM, stride=8), :].astype(BF16)
                two = tail if j == 0 else pltpu.roll(tail, 8 - 2 * j, 0)
                sb[k, j, PM:PP, lanes] = jnp.where(row8 < 2, two, 0.0).astype(BF16)

    def a2a(k, o, b):
        j = tpeer(o)
        return rc(sb.at[k, j, IN[b]], rb.at[k, te, IN[b]], a_s.at[k, o - 1, b], a_r.at[k, o - 1, b], (dp, j))

    def a2a_in(k, o, b):
        j = tpeer(o)
        return rc(sb.at[k, j, IN[b]], rb.at[k, j, IN[b]], a_s.at[k, o - 1, b], a_r.at[k, o - 1, b], (dp, j))

    spread(x, 0)

    pick = pick_matrix(T, PT, PP)
    pick16 = pick.astype(BF16)
    col1 = lax.broadcasted_iota(jnp.int32, (1, PL), 1)
    pad_one = jnp.where(col1 == PT, 1.0, 0.0)
    uplift_col = dot_exact(uplift[...].astype(F32).reshape(1, DSL), pad_one, 0, 0)
    et[te, 0] = (dot(ex[...], pick16, 1, 0) + uplift_col).astype(BF16)
    et[te, 1] = dot(co[...], pick16, 1, 0).astype(BF16)
    off_line = offset[...].astype(F32).reshape(1, PT)
    own_cols = (lax.broadcasted_iota(jnp.int32, (PT, PL), 1) - PP * te) == lax.broadcasted_iota(
        jnp.int32, (PT, PL), 0
    )
    off_row = dot(off_line.astype(BF16), jnp.where(own_cols, 1.0, 0.0).astype(BF16), 1, 0)
    cc[te] = jnp.broadcast_to(off_row, (8, PL))

    pl.semaphore_wait(bar, len(peers))

    tx, t3 = tpeer(2), tpeer(3)

    def wcopy(k, ref, dev):
        return rc(ref, ref, w_s.at[k], w_r.at[k], dev)

    send(wcopy(0, et.at[te, my], x_dev))
    send(wcopy(1, cc.at[te], x_dev))
    for b in range(2):
        for o in (2, 3, 1):
            send(a2a(0, o, b))
    send(wcopy(2, et.at[te], core_dev))
    send(wcopy(3, cc.at[te], core_dev))
    rb[0, te] = sb[0, te]

    lc_ct.wait()
    lc_w1.start()
    lc_w2.start()
    spread(ct, 1)
    for b in range(2):
        for o in (2, 3, 1):
            send(a2a(1, o, b))
    rb[1, te] = sb[1, te]

    wcopy(0, et.at[tx, my], x_dev).wait_recv()
    send(wcopy(4, et.at[tx, my], y_dev))
    wcopy(1, cc.at[tx], x_dev).wait_recv()
    send(wcopy(5, et.at[tx, my], core_dev))
    send(wcopy(6, cc.at[tx], core_dev))
    bias_line = rais[...].astype(F32).reshape(1, HB * NDP)
    for m in range(NDP // 2):
        bias[m : m + 1, :] = bias_line[:, 2 * m * HB : 2 * (m + 1) * HB]
    scaling, centering = scal[...].astype(F32).reshape(1, D), cent[...].astype(F32).reshape(1, D)
    rescaling, recentering = resc[...].astype(F32).reshape(1, D), rece[...].astype(F32).reshape(1, D)
    lowering = lowr[...].astype(F32).reshape(1, D)
    wcopy(4, et.at[tx, 1 - my], y_dev).wait_recv()
    send(wcopy(7, et.at[tx, 1 - my], core_dev))
    tc = tpeer(1)
    for k, ref in ((2, et.at[tc]), (3, cc.at[tc]), (5, et.at[t3, my]), (6, cc.at[t3]), (7, et.at[t3, 1 - my])):
        wcopy(k, ref, core_dev).wait_recv()

    e_t = et[:, 0].reshape(DS, PL)
    c_t = et[:, 1].reshape(DS, PL)
    zero_pad = lax.broadcasted_iota(jnp.int32, (DS, PL), 1) == PT
    e_clean = jnp.where(zero_pad, 0.0, e_t.astype(F32)).astype(BF16)
    off_full = (cc[0] + cc[1]) + (cc[2] + cc[3])
    first8 = lax.broadcasted_iota(jnp.int32, (8, PL), 0) == 0
    off_row8 = jnp.where(first8, off_full, 0.0).astype(BF16)
    ones_row = lax.broadcasted_iota(jnp.int32, (half_r, 1), 0) == PT
    row8d = lax.broadcasted_iota(jnp.int32, (8, D), 0)
    ones8 = jnp.where(row8d == 0, 1.0, 0.0).astype(BF16)

    def image_rows(k, b):
        pieces = []
        for t in range(T):
            tail = rb[k, t, PM:PP, :].astype(F32)
            tail = pltpu.roll(tail, 7, 0) if b else tail
            pieces += [rb[k, t, IMG[b], :].astype(F32), jnp.where(row8d == 0, tail, 0.0)]
        return jnp.concatenate(pieces, axis=0)

    for b in range(2):
        for o in (1, 2, 3):
            a2a_in(0, o, b).wait_recv()
        sl = slice(b * half_r, (b + 1) * half_r)
        xb = image_rows(0, b)
        xhat, _ = norm_stats(xb)
        n = jnp.where(ones_row, 1.0, xhat * scaling + centering).astype(BF16)
        nb16[sl, :] = n
        pre = dot(e_t, n, 1, 0)
        tp[b] = pre
        act, _ = gelu_parts(pre)
        ta[b, 0:DS, :] = act.astype(BF16)
        ta[b, DS : DS + 8, :] = ones8
        mx_b = xb + dot(c_t, ta[b, 0:DS, :], 0, 0) + dot(off_row8, ones8, 0, 0)
        mixed[sl, :] = mx_b
        xh2, _ = norm_stats(mx_b)
        nr[sl, :] = (xh2 * rescaling + recentering).astype(BF16)

    low_sum = jnp.zeros((1, D), F32)
    for b in range(2):
        for o in (1, 2, 3):
            a2a_in(1, o, b).wait_recv()
        sl = slice(b * half_r, (b + 1) * half_r)
        keep = jnp.where(2 * te + b < cnt[0], 1.0, 0.0)
        og = image_rows(1, b) * keep
        ol[sl, :] = og.astype(BF16)
        low_sum = low_sum + jnp.sum(og, axis=0, keepdims=True)
    vv[0] = jnp.zeros(vv.shape[1:], F32)
    vv[0, 4:5, 0:D] = low_sum
    yacc[...] = jnp.zeros(yacc.shape, F32)
    gacc[...] = jnp.zeros(gacc.shape, F32)
    lc_w1.wait()
    lc_w2.wait()

    PR, QR, RR = pl.ds(0, z.P), pl.ds(z.P, z.Q), pl.ds(z.P + z.Q, HC - z.P - z.Q)
    pos = {o: i for i, o in enumerate(ORDER)}

    def add_into(dst, src):
        dst[...] = (dst[...].astype(F32) + src[...].astype(F32)).astype(BF16)

    def flip(m, bit):
        return m + bit - 2 * m * bit

    def piece(o, rows, xx):
        if xx is None:
            return gs.at[pos[o], mc, :, :, rows]
        return gs.at[pos[o], mc, xx, :, rows]

    def core_copy(i):
        return rc(gs.at[i, 1 - mc], r1.at[i], c_s.at[i], c_r.at[i], core_dev)

    def xp_copy(i):
        return rc(gs.at[i, mc, 1 - mx, :, PR], rxp.at[i], xp_s.at[i], xp_r.at[i], x_dev)

    def yq_copy(i):
        k = i // 2
        return rc(gs.at[i, mc, :, :, QR], ryq.at[k], yq_s.at[k], yq_r.at[k], y_dev)

    def ar_copy(i):
        k = i // 4 * 2 + i % 2
        return rc(gs.at[i, mc, :, :, RR], rar.at[k], ar_s.at[k], ar_r.at[k], a_dev)

    def yp_copy(da, db):
        k = 2 * da + db
        return rc(piece((1, da, db), PR, mx), ryp.at[k], yp_s.at[k], yp_r.at[k], y_dev)

    def ap_copy(db):
        return rc(piece((0, 1, db), PR, mx), rap.at[db], ap_s.at[db], ap_r.at[db], a_dev)

    def aq_copy(db):
        return rc(piece((0, 1, db), QR, None), raq.at[db], aq_s.at[db], aq_r.at[db], a_dev)

    def xq_copy(db):
        return rc(piece((0, 0, db), QR, 1 - mx), rxq.at[db], xq_s.at[db], xq_r.at[db], x_dev)

    def yr_copy(db):
        return rc(piece((1, 0, db), RR, None), ryr.at[db], yr_s.at[db], yr_r.at[db], y_dev)

    def xr_copy(db):
        return rc(piece((0, 0, db), RR, 1 - mx), rxr.at[db], xr_s.at[db], xr_r.at[db], x_dev)

    bp_copy = rc(piece((0, 0, 1), PR, mx), rbp, bp_s, bp_r, b_dev)
    bq_copy = rc(piece((0, 0, 1), QR, mx), rbq, bq_s, bq_r, b_dev)
    br_copy = rc(piece((0, 0, 1), RR, mx), rbr, br_s, br_r, b_dev)

    def xp(dy, da, db):
        o = (dy, da, db)
        return xp_copy(pos[o]), o, PR, rxp.at[pos[o]], False, [yp_copy(da, db)] if dy else []

    def yp(da, db):
        return yp_copy(da, db), (0, da, db), PR, ryp.at[2 * da + db], False, [ap_copy(db)] if da else []

    def ap(db):
        return ap_copy(db), (0, 0, db), PR, rap.at[db], False, [bp_copy] if db else []

    def yq(da, db):
        i = pos[1, da, db]
        return yq_copy(i), (0, da, db), QR, ryq.at[i // 2], True, [aq_copy(db)] if da else []

    def aq(db):
        return aq_copy(db), (0, 0, db), QR, raq.at[db], True, [xq_copy(db)]

    def xq(db):
        return xq_copy(db), (0, 0, db), QR, rxq.at[db], False, [bq_copy] if db else []

    def ar(dy, db):
        i = pos[dy, 1, db]
        return ar_copy(i), (dy, 0, db), RR, rar.at[i // 4 * 2 + i % 2], True, [yr_copy(db)] if dy else []

    def yr(db):
        return yr_copy(db), (0, 0, db), RR, ryr.at[db], True, [xr_copy(db)]

    def xr(db):
        return xr_copy(db), (0, 0, db), RR, rxr.at[db], False, [br_copy] if db else []

    steps = dict(xp=xp, yp=yp, ap=ap, yq=yq, aq=aq, xq=xq, ar=ar, yr=yr, xr=xr)

    def take(name, *bits):
        arrival, o, rows, src, both, on = steps[name](*bits)
        arrival.wait_recv()
        for g in range(2):
            if both:
                for xx in range(2):
                    add_into(gs.at[pos[o], mc, xx, g, rows], src.at[xx, g])
            else:
                add_into(gs.at[pos[o], mc, mx, g, rows], src.at[g])
        for c in on:
            c.start()
        return on

    def block(k, carry):
        da, db = 1 - lax.rem(k, 2), 1 - k // 2
        m = flip(mb, db) * 2 + flip(ma, da)
        cols = pl.ds(pl.multiple_of(m * 2 * HB, 2 * HB), 2 * HB)
        pre = dot(nr[...], w1[:, cols], 1, 0) + bias[pl.ds(m, 1), :]
        act, slope = gelu_parts(pre)
        act_s[...] = act.astype(BF16)
        low16 = (slope * dot(ol[...], w2[cols, :], 1, 1)).astype(BF16)
        low_s[...] = low16
        line = jnp.sum(low16.astype(F32), axis=0, keepdims=True)
        for y in range(2):
            vv[0, pl.ds(2 * m + y, 1), D : D + HB] = line[:, y * HB : (y + 1) * HB]
        for h, y in ((0, 1 - my), (1, my)):
            half = pl.ds(pl.multiple_of(y * HB, HB), HB)
            gn = dot(act_s[:, half], ol[...], 0, 0)
            gb = dot(low_s[:, half], nr[...], 0, 0)
            for t in range(T):
                rows = slice(t * HC, (t + 1) * HC)
                gs[2 * k + h, t % 2, t // 2, 0] = gn[rows, :].astype(BF16)
                gs[2 * k + h, t % 2, t // 2, 1] = gb[rows, :].astype(BF16)
            core_copy(2 * k + h).start()
        yacc[...] += dot(act_s[...], w2[cols, :], 1, 0)
        gacc[...] += dot(low_s[...], w1[:, cols], 1, 1)
        for h in range(2):
            i = 2 * k + h
            core_copy(i).wait_recv()
            for xx in range(2):
                for g in range(2):
                    add_into(gs.at[i, mc, xx, g], r1.at[i, xx, g])
            if h == 0:
                yq_copy(i).start()

            @pl.when(da == 1)
            def _():
                ar_copy(i).start()

            xp_copy(i).start()
        for at, ops in EARLY:

            @pl.when(k == at)
            def _():
                for op in ops:
                    take(*op)

        return carry

    lax.fori_loop(0, NDP // 2, block, 0)
    sent.extend([core_copy(i) for i in range(NDP)] + [xp_copy(i) for i in range(NDP)])
    sent.extend([yq_copy(i) for i, o in enumerate(ORDER) if o[0]] + [ar_copy(i) for i, o in enumerate(ORDER) if o[1]])
    for _, ops in EARLY:
        for op in ops:
            sent.extend(steps[op[0]](*op[1:])[-1])

    def ocopy(k, o, b):
        src, dst = (so, ro) if k == 0 else (so2, ro2)
        j = tpeer(o)
        return rc(src.at[j, OUT[b]], dst.at[te, OUT[b]], o_s.at[k, o - 1, b], o_r.at[k, o - 1, b], (dp, j))

    def ocopy_in(k, o, b):
        src, dst = (so, ro) if k == 0 else (so2, ro2)
        j = tpeer(o)
        return rc(src.at[j, OUT[b]], dst.at[j, OUT[b]], o_s.at[k, o - 1, b], o_r.at[k, o - 1, b], (dp, j))

    lc_o = [pltpu.make_async_copy(s.at[te], r.at[te], lsem.at[3 + k]) for k, (s, r) in enumerate(((so, ro), (so2, ro2)))]

    def pack(k, b, t, rows):
        dst = so if k == 0 else so2
        dst[t, IMG[b], :] = rows[0:PM, :].astype(BF16)
        tail = jnp.where(row8d == 0, rows[PM:PP, :], 0.0)
        if b == 0:
            ext[k, t] = tail
        else:
            dst[t, PM:PP, :] = (ext[k, t] + pltpu.roll(tail, 1, 0)).astype(BF16)

    def go(k, b):
        for o in (2, 3, 1):
            send(ocopy(k, o, b))
        if b == 1:
            lc_o[k].start()

    def part(b):
        return slice(b * half_r, (b + 1) * half_r)

    def lo(b):
        keep = jnp.where(2 * te + b < cnt[0], 1.0, 0.0)
        for t in range(T):
            sl = slice(b * half_r + t * PP, b * half_r + (t + 1) * PP)
            pack(0, b, t, (mixed[sl, :] + yacc[sl, :] + lowering) * keep)
        go(0, b)

    def ln2():
        resc_sum = jnp.zeros((1, D), F32)
        rece_sum = jnp.zeros((1, D), F32)
        for b in range(2):
            xh2, rs2 = norm_stats(mixed[part(b), :])
            gr = gacc[part(b), :]
            resc_sum = resc_sum + jnp.sum(gr * xh2, axis=0, keepdims=True)
            rece_sum = rece_sum + jnp.sum(gr, axis=0, keepdims=True)
            mgrad[part(b), :] = ol[part(b), :].astype(F32) + norm_back(gr, xh2, rs2, rescaling)
        vv[0, 2:3, 0:D] = resc_sum
        vv[0, 3:4, 0:D] = rece_sum

    hops = (x_dev, y_dev, a_dev, b_dev)
    e_core = rc(ec.at[1 - mc], ecr, e_s.at[0], e_r.at[0], core_dev)

    def v_copy(s):
        return rc(vv.at[s], vr.at[s], v_s.at[s], v_r.at[s], ((core_dev,) + hops)[s])

    def e_copy(s):
        return rc(es.at[s], er.at[s], e_s.at[s + 1], e_r.at[s + 1], hops[s])

    def tok():
        eg_sum = jnp.zeros((DS, PL), F32)
        cg_sum = jnp.zeros((DS + 8, PL), F32)
        for b in range(2):
            ml = mgrad[part(b), :].astype(BF16)
            _, slope = gelu_parts(tp[b])
            tg = (slope * dot(c_t, ml, 1, 0)).astype(BF16)
            tg16[b] = tg
            cg_sum = cg_sum + dot(ta[b], ml, 1, 1)
            eg_sum = eg_sum + dot(tg, nb16[part(b), :], 1, 1)
        vv[0, 5:6, 0:PL] = cg_sum[DS : DS + 1, :]
        for t in range(T):
            ec[t % 2, t // 2, 0] = eg_sum[t * DSL : (t + 1) * DSL, :]
            ec[t % 2, t // 2, 1] = cg_sum[t * DSL : (t + 1) * DSL, :]
        send(e_core)

    def f(b):
        nback = dot(e_clean, tg16[b], 0, 0)
        xhat, rs1 = norm_stats(image_rows(0, b))
        grad = mgrad[part(b), :] + norm_back(nback, xhat, rs1, scaling)
        for t in range(T):
            pack(1, b, t, grad[t * PP : (t + 1) * PP, :])
        sums[2 * b : 2 * b + 1, :] = jnp.sum(nback * xhat, axis=0, keepdims=True)
        sums[2 * b + 1 : 2 * b + 2, :] = jnp.sum(nback, axis=0, keepdims=True)

    def ig(b):
        go(1, b)

    def e(s):
        if s == 0:
            e_core.wait_recv()
            es[0] = (ec[mc, 1 - mx] + ecr[1 - mx]).astype(BF16)
            send(e_copy(0))
            return
        e_copy(s - 1).wait_recv()
        if s == 1:
            tot = ec[mc, mx] + ecr[mx] + er[0].astype(F32)
        else:
            tot = es[s - 1].astype(F32) + er[s - 1].astype(F32)
        if s == 4:
            ecf[...] = tot
        else:
            es[s] = tot.astype(BF16)
            send(e_copy(s))

    def v(s):
        if s == 0:
            for r in range(2):
                vv[0, r : r + 1, 0:D] = sums[r : r + 1, :] + sums[r + 2 : r + 3, :]
        else:
            v_copy(s - 1).wait_recv()
            vv[s] = vv[s - 1] + vr[s - 1]
        if s < 5:
            send(v_copy(s))

    work = dict(ln2=ln2, tok=tok, f=f, lo=lo, ig=ig, e=e, v=v)
    for op in LATE:
        if op[0] in work:
            work[op[0]](*op[1:])
        else:
            sent.extend(take(*op))

    for copy, rows, buf in ((bq_copy, QR, rbq), (br_copy, RR, rbr), (bp_copy, PR, rbp)):
        copy.wait_recv()
        for g in range(2):
            fin[g, rows, :] = gs[NDP - 1, mc, mx, g, rows, :].astype(F32) + buf[g].astype(F32)
    vec[...] = vv[5]
    for k in range(2):
        for o in (1, 2, 3):
            for b in range(2):
                ocopy_in(k, o, b).wait_recv()
        lc_o[k].wait()

    for c in sent:
        c.wait_send()


def finish_kernel(
    z, ro_h, ro2_h, fin_h, ecf_h, vec_h, lo, ig, eg, up, cg, off, v0, v1, v2, v3, bg, rg, ng, v4,
    xs, ro, ro2, ecf, vec, sem,
):
    D, PT, PP, HB, HC, T, NDP, DSL = z.D, z.PT, z.PP, z.HB, z.HC, z.T, z.NDP, z.DSL
    PM = PT - PT % 8
    te = lax.axis_index("tensor")
    di = lax.rem(lax.axis_index("dp"), NDP)
    pairs = ((ro_h, ro), (ro2_h, ro2), (ecf_h, ecf), (vec_h, vec), (fin_h.at[0], ng), (fin_h.at[1], bg))
    loads = [pltpu.make_async_copy(src, dst, sem.at[k]) for k, (src, dst) in enumerate(pairs)]
    for c in loads:
        c.start()
    for k, (src, dst) in enumerate(((ro, lo), (ro2, ig))):
        loads[k].wait()
        for c in range(D // LANES):
            lanes = slice(c * LANES, (c + 1) * LANES)
            base = c * PT * 8
            for j in range(T):
                for b, at in ((0, 0), (1, PP)):
                    xs[pl.ds(base + 2 * j + b, PM, stride=8), :] = src[j, at : at + PM, lanes].astype(F32)
                last = base + PM * 8 + 2 * j
                xs[last : last + 2, :] = src[j, PM:PP, lanes].astype(F32)[0:2, :]
            dst[:, :, lanes] = xs[base : base + PT * 8, :].reshape(PT, 8, LANES).astype(BF16)
    for c in loads[2:]:
        c.wait()
    pick = pick_matrix(T, PT, PP)
    eg[...] = dot_exact(ecf[0], pick, 1, 1)
    cg[...] = dot_exact(ecf[1], pick, 1, 1)
    row8 = lax.broadcasted_iota(jnp.int32, (8, PP * T), 1)
    up[...] = dot_exact(jnp.where(row8 == PT, 1.0, 0.0), ecf[0], 1, 1)[0:1, :].reshape(DSL)
    for ref, r in ((v0, 0), (v1, 1), (v2, 2), (v3, 3), (v4, 4)):
        ref[...] = vec[r : r + 1, 0:D].reshape(D)
    off_row = vec[5:6, :]
    rg_row = vec[pl.ds(di, 1), D:]
    off_own = jnp.zeros((1, PT), F32)
    rg_own = jnp.zeros((1, HC), F32)
    for t in range(T):
        off_own = off_own + jnp.where(te == t, off_row[:, t * PP : t * PP + PT], 0.0)
        rg_own = rg_own + jnp.where(te == t, rg_row[:, t * HC : (t + 1) * HC], 0.0)
    off[...] = off_own.reshape(PT)
    rg[...] = rg_own.reshape(HC)


def local(
    layer_input, image_counts, expand, uplift, contract, offset, scaling, centering,
    rescaling, recentering, broaden, raising, narrow, lowering, cotangent, *, mesh,
):
    z = Sizes()
    z.PT, images, z.D = layer_input.shape
    z.T, z.NDP = mesh.shape["tensor"], 8
    outer = mesh.shape["dp"] // z.NDP
    z.PP = -(-(z.PT + 1) // 8) * 8
    z.R = 2 * z.T * z.PP
    hidden = broaden.shape[1]
    if outer > 1:
        split = (outer, z.NDP, z.T, hidden // (outer * z.NDP * z.T))
        broaden = broaden.reshape(-1, *split).transpose(0, 2, 3, 1, 4).reshape(-1, hidden)
        raising = raising.reshape(split).transpose(1, 2, 0, 3).reshape(hidden)
        narrow = narrow.reshape(*split, -1).transpose(1, 2, 0, 3, 4).reshape(hidden, -1)
    z.HB = hidden // z.NDP
    z.HC = z.HB // z.T
    z.DSL = expand.shape[1]
    D, T, NDP, PP, PT, R, HB, HC, DSL = z.D, z.T, z.NDP, z.PP, z.PT, z.R, z.HB, z.HC, z.DSL
    DS, PL, PK = DSL * T, PP * T, PP + PT - PT % 8

    vm = pl.BlockSpec(memory_space=pltpu.VMEM)
    anys = pl.BlockSpec(memory_space=pl.ANY)
    dma = pltpu.SemaphoreType.DMA
    V = pltpu.VMEM
    S = jax.ShapeDtypeStruct
    z.P, z.Q = HC * 4 // 12, HC * 4 // 12
    P_, Q_, R_ = z.P, z.Q, HC - z.P - z.Q
    sems = []
    for shape in (
        (2, 3, 2), (8,), (NDP,), (NDP,), (4,), (2,), (), (4,), (2,), (2,), (), (4,), (2,), (2,), (),
        (2, 3, 2), (5,), (5,),
    ):
        sems += [dma(shape), dma(shape)]
    scratch = [
        V((PT, 8, D), BF16), V(broaden.shape, BF16), V(narrow.shape, BF16), V((D // LANES * PT * 8, LANES), F32),
        V((2, T, PK, D), BF16), V((2, T, PK, D), BF16), V((T, 2, DSL, PL), BF16), V((T, 8, PL), F32),
        V((R, D), BF16), V((2, DS, D), F32), V((2, DS + 8, D), BF16), V((R, D), F32), V((R, D), BF16), V((R, D), BF16),
        V((R, D), F32), V((R, D), F32), V((R, D), F32), V((NDP // 2, 2 * HB), F32), V((T, PK, D), BF16), V((T, PK, D), BF16),
        V((2, T, 8, D), F32), V((R, 2 * HB), BF16), V((R, 2 * HB), BF16), V((4, D), F32),
        V((NDP, 2, 2, 2, HC, D), BF16), V((NDP, 2, 2, HC, D), BF16),
        V((NDP, 2, P_, D), BF16), V((4, 2, P_, D), BF16), V((2, 2, P_, D), BF16), V((2, P_, D), BF16),
        V((4, 2, 2, Q_, D), BF16), V((2, 2, 2, Q_, D), BF16), V((2, 2, Q_, D), BF16), V((2, Q_, D), BF16),
        V((4, 2, 2, R_, D), BF16), V((2, 2, 2, R_, D), BF16), V((2, 2, R_, D), BF16), V((2, R_, D), BF16),
        V((6, 8, D + HB), F32), V((5, 8, D + HB), F32), V((2, 2, 2, DSL, PL), F32), V((2, 2, DSL, PL), F32),
        V((4, 2, DSL, PL), BF16), V((4, 2, DSL, PL), BF16), V((2, DS, D), BF16),
        dma((5,)),
    ] + sems
    mid = pl.pallas_call(
        functools.partial(layer_kernel, z),
        out_shape=(
            S((T, PK, D), BF16), S((T, PK, D), BF16), S((2, HC, D), F32), S((2, DSL, PL), F32), S((8, D + HB), F32),
        ),
        in_specs=[pl.BlockSpec(memory_space=pltpu.SMEM), vm, anys] + [vm] * 10 + [anys, anys],
        out_specs=(anys, anys, vm, vm, vm),
        scratch_shapes=scratch,
        compiler_params=pltpu.CompilerParams(
            collective_id=0, has_side_effects=True, vmem_limit_bytes=60 * 1024 * 1024
        ),
    )(
        image_counts, layer_input, cotangent, expand.T, contract, uplift, offset, scaling, centering,
        rescaling, recentering, lowering, raising, broaden, narrow,
    )
    res = pl.pallas_call(
        functools.partial(finish_kernel, z),
        out_shape=(
            S((PT, images, D), BF16), S((PT, images, D), BF16), S((DSL, PT * T), F32), S((DSL,), F32),
            S((DSL, PT * T), F32), S((PT,), F32), S((D,), F32), S((D,), F32), S((D,), F32), S((D,), F32),
            S((HC, D), F32), S((HC,), F32), S((HC, D), F32), S((D,), F32),
        ),
        in_specs=[anys] * 5,
        out_specs=(vm,) * 14,
        scratch_shapes=[
            V((D // LANES * PT * 8, LANES), F32), V((T, PK, D), BF16), V((T, PK, D), BF16), V((2, DSL, PL), F32),
            V((8, D + HB), F32), dma((6,)),
        ],
        compiler_params=pltpu.CompilerParams(vmem_limit_bytes=60 * 1024 * 1024),
    )(*mid)
    lo, ig, eg, up, cg, off, v0, v1, v2, v3, bg, rg, ng, v4 = res
    if outer > 1:
        same = [[o * NDP + i for o in range(outer)] for i in range(NDP)]
        eg, up, cg, off, v0, v1, v2, v3, v4 = lax.psum(
            (eg, up, cg, off, v0, v1, v2, v3, v4), "dp", axis_index_groups=same
        )
        bg, ng, rg = (
            lax.psum_scatter(v, "dp", scatter_dimension=0, axis_index_groups=same, tiled=True) for v in (bg, ng, rg)
        )
    return lo, ig, eg.T, up, cg, off, v0, v1, v2, v3, bg.T, rg, ng, v4


def solution(mesh):
    rows = P("tensor", "dp", None)
    both = ("dp", "tensor")
    in_specs = (
        rows, P("dp"), P(None, "tensor"), P("tensor"), P("tensor", None), P("tensor"),
        P(), P(), P(), P(), P(), P(), P(), P(), rows,
    )
    out_specs = (
        rows, rows, P(None, "tensor"), P("tensor"), P("tensor", None), P("tensor"),
        P(), P(), P(), P(), P(None, both), P(both), P(both, None), P(),
    )
    return jax.shard_map(
        functools.partial(local, mesh=mesh), mesh=mesh, in_specs=in_specs, out_specs=out_specs, check_vma=False
    )
```

time: 91.7 us -> 85.8 us (0.936)
  Pallas kernels: 90.1 us -> 84.1 us
    pallas_call x1, Pallas kernels: 86.6 us -> 80.7 us  [local(): pl.pallas_call(functools.partial(layer_kernel, z), out_shape=(S((T, PK, D...]
where the time goes in v3:
time: 85.8 us; the launch traced here: 85.6 us
  Pallas kernels  84.1 us (98%)
  between operations  1.46 us (2%)
    pallas_call x1, Pallas kernels, local(): pl.pallas_call(functools.partial(layer_kernel, z), out_shape=(S((T, PK, D...  80.7 us
    pallas_call x1, Pallas kernels, local(): pl.pallas_call(functools.partial(finish_kernel, z), out_shape=(S((PT, ima...  3.4 us

profile of v3, /device:TPU:0, one launch (start us, length us, event | category | flops | bytes accessed | tf_op | source)
XLA Modules:
  0.0 85.6 jit_solution(17920943795820772794)
XLA Ops:
  1.3 80.7 %shard_map.254 = (bf16[4,104,768]{2,1,0:T(8,128)(2,1)}, bf16[4,104,768]{2,1,0:T(8,128)(2,1)}, f32[2,96,768]{2,1,0:T(8,128)}, f32[2,96,224]{2,1,0:T(8,128)}, f32[8,1152]{1,0:T(8,128)}) custom-call(s32[1]{0:T(128)S(6)} %copy.29.cnt, bf16[49,8,768]{2,1,0:T(8,128)(2,1)} %x.1, bf16[49,8,768]{2,1,0:T(8,128)(2,1)} %ct_hbm.1, bf16[96,196]{1,0:T(8,128)(2,1)} %bitcast.3, ...), custom_call_target="tpu_custom_call" | custom-call | tf_op jit(solution)/shard_map/pallas_call | solution.py:651
  82.0 3.4 %shard_map.255 = (bf16[49,8,768]{2,1,0:T(8,128)(2,1)}, bf16[49,8,768]{2,1,0:T(8,128)(2,1)}, f32[96,196]{1,0:T(8,128)}, f32[96]{0:T(128)}, f32[96,196]{1,0:T(8,12...) custom-call(bf16[4,104,768]{2,1,0:T(8,128)(2,1)} %get-tuple-element., ...), custom_call_target="tpu_custom_call" | custom-call | tf_op jit(solution)/shard_map/pallas_call | solution.py:666

commit v4 on v3

--- a/solution.py
+++ b/solution.py
@@ -62,25 +62,24 @@
 ORDER = ((1, 1, 1), (0, 1, 1), (1, 0, 1), (0, 0, 1), (1, 1, 0), (0, 1, 0), (1, 0, 0), (0, 0, 0))
 
 EARLY = (
-    (1, (
-        ("yq", 1, 1), ("ar", 1, 1),
+    (2, (
+        ("yq", 1, 1),
     )),
 )
 LATE = (
-    ("yq", 0, 1), ("ar", 0, 1), ("yr", 1), ("ln2",), ("xp", 1, 0, 1), ("tok",), ("xp", 0, 0, 1), ("xp", 1, 1, 1),
-    ("xp", 0, 1, 0), ("f", 0), ("xp", 0, 1, 1), ("aq", 1), ("e", 0), ("lo", 0), ("yq", 1, 0), ("f", 1),
-    ("xp", 1, 1, 0), ("xp", 0, 0, 0), ("xr", 1), ("xq", 1), ("ar", 0, 0), ("v", 0), ("e", 1), ("v", 1), ("ar", 1, 0),
-    ("ig", 0), ("yp", 1, 1), ("e", 2), ("yq", 0, 0), ("aq", 0), ("yp", 0, 1), ("ap", 1), ("yp", 1, 0), ("v", 2),
-    ("lo", 1), ("e", 3), ("v", 3), ("yr", 0), ("xp", 1, 0, 0), ("ig", 1), ("xq", 0), ("v", 4), ("yp", 0, 0),
-    ("v", 5), ("ap", 0), ("xr", 0), ("e", 4),
+    ("lo", 0), ("xp", 1, 0, 1), ("yq", 0, 1), ("ln2",), ("ar", 1, 1), ("xp", 1, 1, 1), ("ar", 0, 1), ("aq", 1),
+    ("tok",), ("f", 0), ("e", 0), ("af", 6), ("xp", 0, 0, 1), ("yq", 1, 0), ("f", 1), ("v", 0), ("xp", 0, 1, 1),
+    ("v", 1), ("e", 1), ("xp", 0, 1, 0), ("xq", 1), ("yr", 1), ("yp", 0, 1), ("yp", 1, 1), ("lo", 1), ("af", 7),
+    ("v", 2), ("ar", 0, 0), ("ar", 1, 0), ("yq", 0, 0), ("xr", 1), ("xp", 1, 1, 0), ("e", 2), ("xp", 1, 0, 0),
+    ("ig", 0), ("ap", 1), ("v", 3), ("aq", 0), ("yr", 0), ("e", 3), ("ig", 1), ("v", 4), ("xp", 0, 0, 0),
+    ("yp", 1, 0), ("yp", 0, 0), ("xq", 0), ("xr", 0), ("ap", 0), ("e", 4), ("v", 5),
 )
-
 
 def layer_kernel(
     z,
-    cnt, x, ct_hbm, ex, co, uplift, offset, scal, cent, resc, rece, lowr, rais, w1_hbm, w2_hbm,
+    cnt, x_hbm, ct_hbm, ex, co, uplift, offset, scal, cent, resc, rece, lowr, rais, w1_hbm, w2_hbm,
     ro, ro2, fin, ecf, vec,
-    ct, w1, w2, xs, sb, rb, et, cc, nb16, tp, ta, mixed, nr, ol, yacc, gacc, mgrad, bias, so, so2, ext, act_s, low_s, sums,
+    x, w1, w2, xs, sb, rb, et, cc, nb16, tp, ta, mixed, nr, ol, yacc, gacc, mgrad, bias, ext, act_s, slope_s, low_s, sums,
     gs, r1, rxp, ryp, rap, rbp, ryq, raq, rxq, rbq, rar, ryr, rxr, rbr,
     vv, vr, ec, ecr, es, er, tg16,
     lsem, a_s, a_r, w_s, w_r, c_s, c_r, xp_s, xp_r, yp_s, yp_r, ap_s, ap_r, bp_s, bp_r,
@@ -125,10 +124,11 @@
         copy.start()
         sent.append(copy)
 
-    lc_ct = pltpu.make_async_copy(ct_hbm, ct, lsem.at[0])
+    lc_ct = pltpu.make_async_copy(ct_hbm, x, lsem.at[0])
     lc_w1 = pltpu.make_async_copy(w1_hbm, w1, lsem.at[1])
     lc_w2 = pltpu.make_async_copy(w2_hbm, w2, lsem.at[2])
-    lc_ct.start()
+    lc_x = pltpu.make_async_copy(x_hbm, x, lsem.at[5])
+    lc_x.start()
 
     peers = [(dp, tpeer(o)) for o in (1, 2, 3)] + [y_dev, a_dev, b_dev]
     bar = pltpu.get_barrier_semaphore()
@@ -161,7 +161,12 @@
         j = tpeer(o)
         return rc(sb.at[k, j, IN[b]], rb.at[k, j, IN[b]], a_s.at[k, o - 1, b], a_r.at[k, o - 1, b], (dp, j))
 
+    lc_x.wait()
     spread(x, 0)
+    lc_ct.start()
+    pl.semaphore_wait(bar, len(peers))
+    for o in (2, 3, 1):
+        a2a(0, o, 0).start()
 
     pick = pick_matrix(T, PT, PP)
     pick16 = pick.astype(BF16)
@@ -177,8 +182,6 @@
     off_row = dot(off_line.astype(BF16), jnp.where(own_cols, 1.0, 0.0).astype(BF16), 1, 0)
     cc[te] = jnp.broadcast_to(off_row, (8, PL))
 
-    pl.semaphore_wait(bar, len(peers))
-
     tx, t3 = tpeer(2), tpeer(3)
 
     def wcopy(k, ref, dev):
@@ -186,9 +189,8 @@
 
     send(wcopy(0, et.at[te, my], x_dev))
     send(wcopy(1, cc.at[te], x_dev))
-    for b in range(2):
-        for o in (2, 3, 1):
-            send(a2a(0, o, b))
+    for o in (2, 3, 1):
+        a2a(0, o, 1).start()
     send(wcopy(2, et.at[te], core_dev))
     send(wcopy(3, cc.at[te], core_dev))
     rb[0, te] = sb[0, te]
@@ -196,10 +198,10 @@
     lc_ct.wait()
     lc_w1.start()
     lc_w2.start()
-    spread(ct, 1)
+    spread(x, 1)
     for b in range(2):
         for o in (2, 3, 1):
-            send(a2a(1, o, b))
+            a2a(1, o, b).start()
     rb[1, te] = sb[1, te]
 
     wcopy(0, et.at[tx, my], x_dev).wait_recv()
@@ -256,6 +258,25 @@
         xh2, _ = norm_stats(mx_b)
         nr[sl, :] = (xh2 * rescaling + recentering).astype(BF16)
 
+    def flip(m, bit):
+        return m + bit - 2 * m * bit
+
+    def pair(k):
+        m = flip(mb, 1 - k // 2) * 2 + flip(ma, 1 - k % 2)
+        return m, pl.ds(pl.multiple_of(m * 2 * HB, 2 * HB), 2 * HB)
+
+    def ahead(k):
+        m, cols = pair(k)
+        act, slope = gelu_parts(dot(nr[...], w1[:, cols], 1, 0) + bias[pl.ds(m, 1), :])
+        act_s[...] = act.astype(BF16)
+        slope_s[...] = slope
+
+    yacc[...] = jnp.zeros(yacc.shape, F32)
+    gacc[...] = jnp.zeros(gacc.shape, F32)
+    vv[0] = jnp.zeros(vv.shape[1:], F32)
+    lc_w1.wait()
+    lc_w2.wait()
+    ahead(0)
     low_sum = jnp.zeros((1, D), F32)
     for b in range(2):
         for o in (1, 2, 3):
@@ -265,21 +286,13 @@
         og = image_rows(1, b) * keep
         ol[sl, :] = og.astype(BF16)
         low_sum = low_sum + jnp.sum(og, axis=0, keepdims=True)
-    vv[0] = jnp.zeros(vv.shape[1:], F32)
     vv[0, 4:5, 0:D] = low_sum
-    yacc[...] = jnp.zeros(yacc.shape, F32)
-    gacc[...] = jnp.zeros(gacc.shape, F32)
-    lc_w1.wait()
-    lc_w2.wait()
 
     PR, QR, RR = pl.ds(0, z.P), pl.ds(z.P, z.Q), pl.ds(z.P + z.Q, HC - z.P - z.Q)
     pos = {o: i for i, o in enumerate(ORDER)}
 
     def add_into(dst, src):
         dst[...] = (dst[...].astype(F32) + src[...].astype(F32)).astype(BF16)
-
-    def flip(m, bit):
-        return m + bit - 2 * m * bit
 
     def piece(o, rows, xx):
         if xx is None:
@@ -368,58 +381,60 @@
             c.start()
         return on
 
-    def block(k, carry):
-        da, db = 1 - lax.rem(k, 2), 1 - k // 2
-        m = flip(mb, db) * 2 + flip(ma, da)
-        cols = pl.ds(pl.multiple_of(m * 2 * HB, 2 * HB), 2 * HB)
-        pre = dot(nr[...], w1[:, cols], 1, 0) + bias[pl.ds(m, 1), :]
-        act, slope = gelu_parts(pre)
-        act_s[...] = act.astype(BF16)
-        low16 = (slope * dot(ol[...], w2[cols, :], 1, 1)).astype(BF16)
+    def af(i):
+        core_copy(i).wait_recv()
+        for xx in range(2):
+            for g in range(2):
+                add_into(gs.at[i, mc, xx, g], r1.at[i, xx, g])
+
+    def first_hops(i):
+        dy, da, _ = ORDER[i]
+        if dy:
+            yq_copy(i).start()
+        if da:
+            ar_copy(i).start()
+        xp_copy(i).start()
+
+    for k in range(NDP // 2):
+        m, cols = pair(k)
+        low16 = (slope_s[...] * dot(ol[...], w2[cols, :], 1, 1)).astype(BF16)
         low_s[...] = low16
         line = jnp.sum(low16.astype(F32), axis=0, keepdims=True)
         for y in range(2):
             vv[0, pl.ds(2 * m + y, 1), D : D + HB] = line[:, y * HB : (y + 1) * HB]
-        for h, y in ((0, 1 - my), (1, my)):
-            half = pl.ds(pl.multiple_of(y * HB, HB), HB)
-            gn = dot(act_s[:, half], ol[...], 0, 0)
-            gb = dot(low_s[:, half], nr[...], 0, 0)
+        if k > 0:
+            for i in (2 * k - 2, 2 * k - 1):
+                af(i)
+                first_hops(i)
+        gn = dot(act_s[...], ol[...], 0, 0)
+        gb = dot(low_s[...], nr[...], 0, 0)
+        for y, h in ((0, 1 - my), (1, my)):
             for t in range(T):
-                rows = slice(t * HC, (t + 1) * HC)
+                rows = slice(y * HB + t * HC, y * HB + (t + 1) * HC)
                 gs[2 * k + h, t % 2, t // 2, 0] = gn[rows, :].astype(BF16)
                 gs[2 * k + h, t % 2, t // 2, 1] = gb[rows, :].astype(BF16)
+        for h in range(2):
             core_copy(2 * k + h).start()
         yacc[...] += dot(act_s[...], w2[cols, :], 1, 0)
         gacc[...] += dot(low_s[...], w1[:, cols], 1, 1)
-        for h in range(2):
-            i = 2 * k + h
-            core_copy(i).wait_recv()
-            for xx in range(2):
-                for g in range(2):
-                    add_into(gs.at[i, mc, xx, g], r1.at[i, xx, g])
-            if h == 0:
-                yq_copy(i).start()
-
-            @pl.when(da == 1)
-            def _():
-                ar_copy(i).start()
-
-            xp_copy(i).start()
+        if k + 1 < NDP // 2:
+            ahead(k + 1)
         for at, ops in EARLY:
-
-            @pl.when(k == at)
-            def _():
+            if at == k:
                 for op in ops:
                     take(*op)
 
-        return carry
-
-    lax.fori_loop(0, NDP // 2, block, 0)
     sent.extend([core_copy(i) for i in range(NDP)] + [xp_copy(i) for i in range(NDP)])
     sent.extend([yq_copy(i) for i, o in enumerate(ORDER) if o[0]] + [ar_copy(i) for i, o in enumerate(ORDER) if o[1]])
     for _, ops in EARLY:
         for op in ops:
             sent.extend(steps[op[0]](*op[1:])[-1])
+
+    so, so2 = sb.at[0], sb.at[1]
+    for k in range(2):
+        for o in (1, 2, 3):
+            for b in range(2):
+                a2a(k, o, b).wait_send()
 
     def ocopy(k, o, b):
         src, dst = (so, ro) if k == 0 else (so2, ro2)
@@ -534,7 +549,11 @@
         if s < 5:
             send(v_copy(s))
 
-    work = dict(ln2=ln2, tok=tok, f=f, lo=lo, ig=ig, e=e, v=v)
+    def last_block(i):
+        af(i)
+        first_hops(i)
+
+    work = dict(af=last_block, ln2=ln2, tok=tok, f=f, lo=lo, ig=ig, e=e, v=v)
     for op in LATE:
         if op[0] in work:
             work[op[0]](*op[1:])
@@ -638,26 +657,26 @@
         V((PT, 8, D), BF16), V(broaden.shape, BF16), V(narrow.shape, BF16), V((D // LANES * PT * 8, LANES), F32),
         V((2, T, PK, D), BF16), V((2, T, PK, D), BF16), V((T, 2, DSL, PL), BF16), V((T, 8, PL), F32),
         V((R, D), BF16), V((2, DS, D), F32), V((2, DS + 8, D), BF16), V((R, D), F32), V((R, D), BF16), V((R, D), BF16),
-        V((R, D), F32), V((R, D), F32), V((R, D), F32), V((NDP // 2, 2 * HB), F32), V((T, PK, D), BF16), V((T, PK, D), BF16),
-        V((2, T, 8, D), F32), V((R, 2 * HB), BF16), V((R, 2 * HB), BF16), V((4, D), F32),
+        V((R, D), F32), V((R, D), F32), V((R, D), F32), V((NDP // 2, 2 * HB), F32),
+        V((2, T, 8, D), F32), V((R, 2 * HB), BF16), V((R, 2 * HB), F32), V((R, 2 * HB), BF16), V((4, D), F32),
         V((NDP, 2, 2, 2, HC, D), BF16), V((NDP, 2, 2, HC, D), BF16),
         V((NDP, 2, P_, D), BF16), V((4, 2, P_, D), BF16), V((2, 2, P_, D), BF16), V((2, P_, D), BF16),
         V((4, 2, 2, Q_, D), BF16), V((2, 2, 2, Q_, D), BF16), V((2, 2, Q_, D), BF16), V((2, Q_, D), BF16),
         V((4, 2, 2, R_, D), BF16), V((2, 2, 2, R_, D), BF16), V((2, 2, R_, D), BF16), V((2, R_, D), BF16),
         V((6, 8, D + HB), F32), V((5, 8, D + HB), F32), V((2, 2, 2, DSL, PL), F32), V((2, 2, DSL, PL), F32),
         V((4, 2, DSL, PL), BF16), V((4, 2, DSL, PL), BF16), V((2, DS, D), BF16),
-        dma((5,)),
+        dma((6,)),
     ] + sems
     mid = pl.pallas_call(
         functools.partial(layer_kernel, z),
         out_shape=(
             S((T, PK, D), BF16), S((T, PK, D), BF16), S((2, HC, D), F32), S((2, DSL, PL), F32), S((8, D + HB), F32),
         ),
-        in_specs=[pl.BlockSpec(memory_space=pltpu.SMEM), vm, anys] + [vm] * 10 + [anys, anys],
+        in_specs=[pl.BlockSpec(memory_space=pltpu.SMEM), anys, anys] + [vm] * 10 + [anys, anys],
         out_specs=(anys, anys, vm, vm, vm),
         scratch_shapes=scratch,
         compiler_params=pltpu.CompilerParams(
-            collective_id=0, has_side_effects=True, vmem_limit_bytes=60 * 1024 * 1024
+            collective_id=0, has_side_effects=True, vmem_limit_bytes=62 * 1024 * 1024
         ),
     )(
         image_counts, layer_input, cotangent, expand.T, contract, uplift, offset, scaling, centering,

time: 85.8 us -> 80 us (0.932)
  Pallas kernels: 84.1 us -> 78.3 us
    pallas_call x1, Pallas kernels: 80.7 us -> 74.9 us  [local(): pl.pallas_call(functools.partial(layer_kernel, z), out_shape=(S((T, PK, D...]
where the time goes in v4:
time: 80 us; the launch traced here: 79.8 us
  Pallas kernels  78.3 us (98%)
  between operations  1.46 us (2%)
    pallas_call x1, Pallas kernels, local(): pl.pallas_call(functools.partial(layer_kernel, z), out_shape=(S((T, PK, D...  74.9 us
    pallas_call x1, Pallas kernels, local(): pl.pallas_call(functools.partial(finish_kernel, z), out_shape=(S((PT, ima...  3.4 us

profile of v4, /device:TPU:0, one launch (start us, length us, event | category | flops | bytes accessed | tf_op | source)
XLA Modules:
  0.0 79.8 jit_solution(13594998091250502797)
XLA Ops:
  1.3 74.9 %shard_map.254 = (bf16[4,104,768]{2,1,0:T(8,128)(2,1)}, bf16[4,104,768]{2,1,0:T(8,128)(2,1)}, f32[2,96,768]{2,1,0:T(8,128)}, f32[2,96,224]{2,1,0:T(8,128)}, f32[8,1152]{1,0:T(8,128)}) custom-call(s32[1]{0:T(128)S(6)} %copy.29.cnt, bf16[49,8,768]{2,1,0:T(8,128)(2,1)} %x_hbm.1, bf16[49,8,768]{2,1,0:T(8,128)(2,1)} %ct_hbm.1, bf16[96,196]{1,0:T(8,128)(2,1)} %bitcast.3, ...), custom_call_target="tpu_custom_call" | custom-call | tf_op jit(solution)/shard_map/pallas_call | solution.py:670
  76.2 3.4 %shard_map.255 = (bf16[49,8,768]{2,1,0:T(8,128)(2,1)}, bf16[49,8,768]{2,1,0:T(8,128)(2,1)}, f32[96,196]{1,0:T(8,128)}, f32[96]{0:T(128)}, f32[96,196]{1,0:T(8,12...) custom-call(bf16[4,104,768]{2,1,0:T(8,128)(2,1)} %get-tuple-element., ...), custom_call_target="tpu_custom_call" | custom-call | tf_op jit(solution)/shard_map/pallas_call | solution.py:685

commit v5 on v4

--- a/solution.py
+++ b/solution.py
@@ -67,12 +67,12 @@
     )),
 )
 LATE = (
-    ("lo", 0), ("xp", 1, 0, 1), ("yq", 0, 1), ("ln2",), ("ar", 1, 1), ("xp", 1, 1, 1), ("ar", 0, 1), ("aq", 1),
-    ("tok",), ("f", 0), ("e", 0), ("af", 6), ("xp", 0, 0, 1), ("yq", 1, 0), ("f", 1), ("v", 0), ("xp", 0, 1, 1),
-    ("v", 1), ("e", 1), ("xp", 0, 1, 0), ("xq", 1), ("yr", 1), ("yp", 0, 1), ("yp", 1, 1), ("lo", 1), ("af", 7),
-    ("v", 2), ("ar", 0, 0), ("ar", 1, 0), ("yq", 0, 0), ("xr", 1), ("xp", 1, 1, 0), ("e", 2), ("xp", 1, 0, 0),
-    ("ig", 0), ("ap", 1), ("v", 3), ("aq", 0), ("yr", 0), ("e", 3), ("ig", 1), ("v", 4), ("xp", 0, 0, 0),
-    ("yp", 1, 0), ("yp", 0, 0), ("xq", 0), ("xr", 0), ("ap", 0), ("e", 4), ("v", 5),
+    ("xp", 1, 1, 1), ("lo", 0), ("ln2",), ("tok",), ("f", 0), ("yq", 0, 1), ("xp", 1, 0, 1), ("xp", 0, 0, 1),
+    ("f", 1), ("af", 6), ("v", 0), ("v", 1), ("e", 0), ("xp", 0, 1, 1), ("ig", 0), ("ar", 1, 1), ("yp", 1, 1),
+    ("aq", 1), ("v", 2), ("yp", 0, 1), ("e", 1), ("af", 7), ("ar", 0, 1), ("ap", 1), ("lo", 1), ("yq", 1, 0),
+    ("ar", 1, 0), ("xp", 1, 0, 0), ("xq", 1), ("v", 3), ("ar", 0, 0), ("yq", 0, 0), ("xp", 1, 1, 0), ("xp", 0, 1, 0),
+    ("yr", 1), ("yr", 0), ("e", 2), ("aq", 0), ("xr", 1), ("v", 4), ("xp", 0, 0, 0), ("yp", 1, 0), ("ig", 1),
+    ("yp", 0, 0), ("e", 3), ("v", 5), ("ap", 0), ("xr", 0), ("e", 4), ("xq", 0),
 )
 
 def layer_kernel(
@@ -485,7 +485,7 @@
         vv[0, 2:3, 0:D] = resc_sum
         vv[0, 3:4, 0:D] = rece_sum
 
-    hops = (x_dev, y_dev, a_dev, b_dev)
+    hops = (x_dev, b_dev, a_dev, y_dev)
     e_core = rc(ec.at[1 - mc], ecr, e_s.at[0], e_r.at[0], core_dev)
 
     def v_copy(s):

time: 80 us -> 79.7 us (level)
  no operation moved by 1% of the time
where the time goes in v5:
time: 79.7 us; the launch traced here: 79.4 us
  Pallas kernels  77.9 us (98%)
  between operations  1.46 us (2%)
    pallas_call x1, Pallas kernels, local(): pl.pallas_call(functools.partial(layer_kernel, z), out_shape=(S((T, PK, D...  74.5 us
    pallas_call x1, Pallas kernels, local(): pl.pallas_call(functools.partial(finish_kernel, z), out_shape=(S((PT, ima...  3.4 us

profile of v5, /device:TPU:0, one launch (start us, length us, event | category | flops | bytes accessed | tf_op | source)
XLA Modules:
  0.0 79.4 jit_solution(14890690521299478127)
XLA Ops:
  1.3 74.5 %shard_map.254 = (bf16[4,104,768]{2,1,0:T(8,128)(2,1)}, bf16[4,104,768]{2,1,0:T(8,128)(2,1)}, f32[2,96,768]{2,1,0:T(8,128)}, f32[2,96,224]{2,1,0:T(8,128)}, f32[8,1152]{1,0:T(8,128)}) custom-call(s32[1]{0:T(128)S(6)} %copy.29.cnt, bf16[49,8,768]{2,1,0:T(8,128)(2,1)} %x_hbm.1, bf16[49,8,768]{2,1,0:T(8,128)(2,1)} %ct_hbm.1, bf16[96,196]{1,0:T(8,128)(2,1)} %bitcast.3, ...), custom_call_target="tpu_custom_call" | custom-call | tf_op jit(solution)/shard_map/pallas_call | solution.py:670
  75.8 3.4 %shard_map.255 = (bf16[49,8,768]{2,1,0:T(8,128)(2,1)}, bf16[49,8,768]{2,1,0:T(8,128)(2,1)}, f32[96,196]{1,0:T(8,128)}, f32[96]{0:T(128)}, f32[96,196]{1,0:T(8,12...) custom-call(bf16[4,104,768]{2,1,0:T(8,128)(2,1)} %get-tuple-element., ...), custom_call_target="tpu_custom_call" | custom-call | tf_op jit(solution)/shard_map/pallas_call | solution.py:685
